TPU v7x, 32 devices: a whole 2x2x4 slice. The times are simulated.
32 devices in a mesh: lat: 8 (over z, y), lev: 4 (over x, core).
Axes of the slice: x: 2, y: 2, z: 4, core: 2. Of those that a mesh axis runs over, the one named last changes fastest.
Arguments:
- spec_in: bfloat16 [192, 171, 4, 512], P('lat', None, None, 'lev'), may hold values from -6 to 6
- cotangent: bfloat16 [192, 171, 4, 512], P('lat', None, None, 'lev'), may hold values from -6 to 6
- legendre: bfloat16 [192, 171, 256], P('lat'), may hold values from -0.4375 to 0.4375
- quad_weights: float32 [256], replicated, may hold values from 0.5 to 2
- wave_order: int32 [192], replicated, may hold values from 0 to 191, each once
- norm_gain: float32 [256], replicated, may hold values from 0.5 to 1.5
- weight_in: bfloat16 [256, 512], replicated, may hold values from -0.375 to 0.375
- bias_in: float32 [512], replicated, may hold values from -3 to 3
- weight_mid: bfloat16 [512, 512], replicated, may hold values from -0.25 to 0.25
- bias_mid: float32 [512], replicated, may hold values from -3 to 3
- weight_out: bfloat16 [512, 256], replicated, may hold values from -0.25 to 0.25
Outputs:
- grad_spec: float32 [192, 171, 4, 512], P('lat', None, None, 'lev')
- grad_gain: float32 [256], replicated
- grad_w_in: float32 [256, 512], replicated
- grad_b_in: float32 [512], replicated
- grad_w_mid: float32 [512, 512], replicated
- grad_b_mid: float32 [512], replicated
- grad_w_out: float32 [512, 256], replicated
Inputs may be any that keep to these rules, and one draw needn't show every extreme that they name: `wave_order`: each of 0 to 191 appears once; a slot holding 171 or more is unused.
All inputs are finite; a program needn't handle non-finite values.
Results may differ from a plain program's by a relative error of at most 0.007.
Values may be sent and summed in bfloat16 or wider, within the bound.
No kernel may reach another device: no remote copies, remote signals or barrier semaphores. Data moves between devices by JAX's collectives and lax.ppermute only.
A program may use at most 256 MiB of HBM per device.

v0:
```python
import math

import jax
import jax.numpy as jnp
from jax import lax
from jax.sharding import PartitionSpec as P

WAVES = 171
NLAT = 256
NLON = 512
MEMBERS = 4


time_step = 0.5
norm_eps = 1e-06


def spectral_masks(waves_held, degree_count):
    degree = jnp.arange(degree_count, dtype=jnp.int32)
    living = (waves_held[:, None] <= degree[None, :]) & (waves_held[:, None] < WAVES)
    ratio = (degree * (degree + 1)).astype(jnp.float32) / float(WAVES * (WAVES - 1))
    factor = 1.0 / (1.0 + ratio * ratio)
    shrink = jnp.where(living, factor[None, :], jnp.zeros_like(factor)[None, :])
    return (living, shrink)


def fourier_table(waves_all):
    longitude = jnp.arange(NLON, dtype=jnp.int32)
    phase_steps = waves_all[:, None] * longitude[None, :] % NLON
    angles = phase_steps.astype(jnp.float32) * (2.0 * math.pi / NLON)
    weight_scale = jnp.where(waves_all < WAVES, math.sqrt(2.0 / NLON), 0.0).astype(jnp.float32)[
        :, None
    ]
    return jnp.stack(
        [jnp.cos(angles) * weight_scale, -jnp.sin(angles) * weight_scale], axis=1
    ).astype(jnp.bfloat16)


def contract_rows(left, right):
    return lax.dot_general(
        left, right, (((0,), (0,)), ((), ())), preferred_element_type=jnp.float32
    )


def contract_cols(left, right):
    return lax.dot_general(
        left, right, (((1,), (1,)), ((), ())), preferred_element_type=jnp.float32
    )


def column_grads(
    columns, column_cot, norm_gain, weight_in, bias_in, weight_mid, bias_mid, weight_out
):
    inputs = columns.astype(jnp.float32)
    inverse = lax.rsqrt(jnp.mean(inputs * inputs, axis=1, keepdims=True) + norm_eps)
    normed = (inputs * inverse * norm_gain).astype(jnp.bfloat16)
    pre_one = jnp.dot(normed, weight_in, preferred_element_type=jnp.float32) + bias_in
    sig_one = jax.nn.sigmoid(pre_one)
    act_one = (pre_one * sig_one).astype(jnp.bfloat16)
    pre_two = jnp.dot(act_one, weight_mid, preferred_element_type=jnp.float32) + bias_mid
    sig_two = jax.nn.sigmoid(pre_two)
    act_two = (pre_two * sig_two).astype(jnp.bfloat16)
    gradient_third = contract_rows(act_two, column_cot)
    back_two = contract_cols(column_cot, weight_out)
    delta_two = (back_two * sig_two * (1.0 + pre_two * (1.0 - sig_two))).astype(jnp.bfloat16)
    gradient_second = contract_rows(act_one, delta_two)
    offset_second = jnp.sum(delta_two.astype(jnp.float32), axis=0)
    back_one = contract_cols(delta_two, weight_mid)
    delta_one = (back_one * sig_one * (1.0 + pre_one * (1.0 - sig_one))).astype(jnp.bfloat16)
    gradient_first = contract_rows(normed, delta_one)
    offset_first = jnp.sum(delta_one.astype(jnp.float32), axis=0)
    back_norm = contract_cols(delta_one, weight_in)
    gradient_gain = jnp.sum(back_norm * inputs * inverse, axis=0)
    scaled = back_norm * norm_gain
    grad_columns = inverse * scaled - inputs * inverse * inverse * inverse * jnp.mean(
        scaled * inputs, axis=1, keepdims=True
    )
    return (
        grad_columns.astype(jnp.bfloat16),
        (
            gradient_gain,
            gradient_first,
            offset_first,
            gradient_second,
            offset_second,
            gradient_third,
        ),
    )


def synthesize(wave_table, coeffs):
    shape = coeffs.shape
    split = coeffs.reshape(shape[0], shape[1], shape[2], shape[3] // 2, 2)
    return jnp.einsum(
        "spo,stecp->otec", wave_table, split, preferred_element_type=jnp.float32
    ).astype(jnp.bfloat16)


def analyze(wave_table, values):
    result = jnp.einsum(
        "spo,otec->stecp", wave_table, values, preferred_element_type=jnp.float32
    ).astype(jnp.bfloat16)
    shape = result.shape
    return result.reshape(shape[0], shape[1], shape[2], shape[3] * 2)


def local(
    spec_in,
    cotangent,
    legendre,
    quad_weights,
    wave_order,
    norm_gain,
    weight_in,
    bias_in,
    weight_mid,
    bias_mid,
    weight_out,
):
    slots_here = spec_in.shape[0]
    lat_count = lax.axis_size("lat")
    lev_count = lax.axis_size("lev")
    own_waves = lax.dynamic_slice_in_dim(wave_order, lax.axis_index("lat") * slots_here, slots_here)
    living, shrink = spectral_masks(own_waves, spec_in.shape[1])
    basis_rows = jnp.where(living[:, :, None], legendre, jnp.zeros_like(legendre))
    wave_table = fourier_table(wave_order)
    fourier = jnp.einsum(
        "slt,slek->stek", basis_rows, spec_in, preferred_element_type=jnp.float32
    ).astype(jnp.bfloat16)
    pushed = (time_step * cotangent.astype(jnp.float32) * shrink[:, :, None, None]).astype(
        jnp.bfloat16
    )
    pulled = jnp.einsum("slt,slek->stek", basis_rows, pushed, preferred_element_type=jnp.float32)
    pulled = (quad_weights[None, :, None, None] * pulled).astype(jnp.bfloat16)
    members = spec_in.shape[2]
    packed_part = spec_in.shape[3]
    fourier_all, pulled_all = (
        lax.all_to_all(fourier, ("lat", "lev"), split_axis=1, concat_axis=0, tiled=True),
        lax.all_to_all(pulled, ("lat", "lev"), split_axis=1, concat_axis=0, tiled=True),
    )
    rows_here = fourier_all.shape[1]

    def regroup(received):
        shaped = received.reshape(lat_count, lev_count, slots_here, rows_here, members, packed_part)
        shaped = jnp.transpose(shaped, (0, 2, 3, 4, 1, 5))
        return shaped.reshape(lat_count * slots_here, rows_here, members, lev_count * packed_part)

    grid_values = synthesize(wave_table, regroup(fourier_all))
    grid_cot = synthesize(wave_table, regroup(pulled_all))
    grid_shape = grid_values.shape
    grad_rows, grads_local = column_grads(
        grid_values.reshape(-1, grid_shape[3]),
        grid_cot.reshape(-1, grid_shape[3]),
        norm_gain,
        weight_in,
        bias_in,
        weight_mid,
        bias_mid,
        weight_out,
    )
    grad_grid = grad_rows.reshape(grid_shape)
    back_fourier = analyze(wave_table, grad_grid)
    rows_here = back_fourier.shape[1]
    shaped = back_fourier.reshape(lat_count, slots_here, rows_here, members, lev_count, packed_part)
    shaped = jnp.transpose(shaped, (0, 4, 1, 2, 3, 5))
    shaped = shaped.reshape(lat_count * lev_count * slots_here, rows_here, members, packed_part)
    back_slots = lax.all_to_all(shaped, ("lat", "lev"), split_axis=0, concat_axis=1, tiled=True)
    summed = lax.psum(
        (
            grads_local[0],
            grads_local[1],
            grads_local[2],
            grads_local[3],
            grads_local[4],
            grads_local[5],
        ),
        ("lat", "lev"),
    )
    factor = float(MEMBERS * NLAT * NLON) ** (-0.5)
    grads = tuple((piece * factor for piece in summed))
    grad_spec = cotangent.astype(jnp.float32) * shrink[:, :, None, None] + jnp.einsum(
        "slt,stek->slek", basis_rows, back_slots, preferred_element_type=jnp.float32
    )
    return (grad_spec, grads[0], grads[1], grads[2], grads[3], grads[4], grads[5])


def solution(mesh):
    placed = (
        P("lat", None, None, "lev"),
        P("lat", None, None, "lev"),
        P("lat", None, None),
        P(),
        P(),
        P(),
        P(),
        P(),
        P(),
        P(),
        P(),
    )
    return jax.shard_map(
        local,
        mesh=mesh,
        in_specs=placed,
        out_specs=(P("lat", None, None, "lev"), P(), P(), P(), P(), P(), P()),
        check_vma=False,
    )
```

profile of v0, /device:TPU:0, one launch (start us, length us, event | category | flops | bytes accessed | tf_op | source)
XLA Modules:
  0.0 1022.6 jit_solution(4647882356765720016)
XLA Ops:
  7.2 0.0 copy-start
  7.2 0.8 broadcast_compare_fusion
  8.0 0.1 fusion.39
  8.1 0.1 copy.105
  8.2 2.7 select_bitcast_fusion
  11.0 0.0 copy-start.23
  11.0 7.6 fusion.21
  18.6 10.3 %copy.108 = bf16[24,256,4,128]{3,2,0,1:T(4,128)(2,1)} copy(bf16[24,256,4,128]{3,1,2,0:T(8,128)(2,1)} %fusion.21) | data formatting | bytes 12582912 | tf_op jit(solution)/shard_map/convert_element_type | solution.py:129
  28.9 7.7 all-to-all-start
  36.5 0.7 broadcast_multiply_fusion.4
  37.2 0.0 copy-done.23
  37.2 6.5 multiply_convert_fusion.6
  43.7 10.3 %copy.116 = bf16[24,256,4,128]{3,2,0,1:T(4,128)(2,1)} copy(bf16[24,256,4,128]{3,1,2,0:T(8,128)(2,1)} %multiply_convert_fusion.6) | data formatting | bytes 12582912 | tf_op jit(solution)/shard_map/convert_element_type | solution.py:134
  54.0 122.3 %all-to-all-done = bf16[24,256,4,128]{3,2,0,1:T(4,128)(2,1)} async-done(((bf16[24,256,4,128]{3,2,0,1:T(4,128)(2,1)}), bf16[24,256,4,128]{3,2,0,1:T(4,128)(2,1)}, u32[]{:S(2)}, u32[]{:S(2)}) %all-to-all-start) | async-done | bytes 6291488 | tf_op jit(solution)/shard_map/all_to_all | solution.py:138
  176.3 3.9 all-to-all-start.1
  180.2 0.0 copy-done.15
  180.2 1.9 multiply_convert_fusion.8
  182.1 0.0 copy-start.8
  182.1 0.0 copy-start.10
  182.1 8.1 copy.109
  190.2 55.3 %copy.111 = bf16[8,24,8,4,4,128]{1,0,2,5,4,3:T(8,128)(2,1)} copy(bf16[8,24,8,4,4,128]{5,2,4,0,3,1:T(8,128)(2,1)} %bitcast.75) | data formatting | bytes 12582912 | tf_op jit(solution)/shard_map/transpose | solution.py:145
  245.5 39.0 %reshape_reshape.9 = bf16[192,8,4,256,2]{0,1,4,3,2:T(8,128)(2,1)} reshape(bf16[8,24,8,4,4,128]{1,0,2,5,4,3:T(8,128)(2,1)} %copy.111) | data formatting | bytes 12582912 | tf_op jit(solution)/shard_map/reshape;reshape | solution.py:93
  284.5 21.8 %multiply_reduce_fusion.2 = (f32[512,8,4]{0,2,1:T(4,128)S(1)}, f32[512,8,4,256]{3,0,2,1:T(8,128)}) fusion(bf16[192,8,4,256,2]{0,1,4,3,2:T(8,128)(2,1)} %reshape_reshape.9, bf16[192,1,512]{2,0,1:T(8,128)(2,1)S(1)} %get-tuple-element.62, bf16[192,1,512]{2,0,1:T(8,128)(2,1)S(1)} %get-tuple-element.61), kind=kOutput, calls=%fused_computation.14 | convolution fusion | flops 3238772736 | bytes 23527424 | tf_op jit(solution)/shard_map/spo,stecp->otec/dot_general | solution.py:94
  306.3 0.8 copy.114
  307.1 1.6 rsqrt.12
  308.8 20.9 %copy.122 = f32[512,8,4,256]{3,2,1,0:T(4,128)} copy(f32[512,8,4,256]{3,0,2,1:T(8,128)} %get-tuple-element.64) | data formatting | bytes 33554432 | tf_op jit(solution)/shard_map/convert_element_type | solution.py:54
  329.7 19.6 %reshape.296 = f32[16384,256]{1,0:T(8,128)} reshape(f32[512,8,4,256]{3,2,1,0:T(4,128)} %copy.122) | data formatting | bytes 33554432 | tf_op jit(solution)/shard_map/convert_element_type | solution.py:54
  349.3 0.0 all-to-all-done.1
  349.3 7.9 copy.117
  357.2 55.3 %copy.119 = bf16[8,24,8,4,4,128]{1,0,2,5,4,3:T(8,128)(2,1)} copy(bf16[8,24,8,4,4,128]{5,2,4,0,3,1:T(8,128)(2,1)} %bitcast.76) | data formatting | bytes 12582912 | tf_op jit(solution)/shard_map/transpose | solution.py:145
  412.5 39.0 %reshape_reshape.10 = bf16[192,8,4,256,2]{0,1,4,3,2:T(8,128)(2,1)} reshape(bf16[8,24,8,4,4,128]{1,0,2,5,4,3:T(8,128)(2,1)} %copy.119) | data formatting | bytes 12582912 | tf_op jit(solution)/shard_map/reshape;reshape | solution.py:93
  451.5 0.0 copy-done.10
  451.5 17.2 %bitcast_convert_fusion = bf16[512,8,4,256]{3,0,2,1:T(8,128)(2,1)} fusion(bf16[192,8,4,256,2]{0,1,4,3,2:T(8,128)(2,1)} %reshape_reshape.10, bf16[192,1,512]{2,0,1:T(8,128)(2,1)S(1)} %get-tuple-element.62, bf16[192,1,512]{2,0,1:T(8,128)(2,1)S(1)} %get-tuple-element.61), kind=kOutput, calls=%fused_computation.8 | convolution fusion | flops 3226206208 | bytes 15073280 | tf_op jit(solution)/shard_map/spo,stecp->otec/dot_general | solution.py:94
  468.7 12.4 %copy.121 = bf16[512,8,4,256]{3,2,1,0:T(4,128)(2,1)} copy(bf16[512,8,4,256]{3,0,2,1:T(8,128)(2,1)} %bitcast_convert_fusion) | data formatting | bytes 16777216 | tf_op jit(solution)/shard_map/convert_element_type | solution.py:96
  481.0 12.6 %reshape.293 = bf16[16384,256]{1,0:T(8,128)(2,1)} reshape(bf16[512,8,4,256]{3,2,1,0:T(4,128)(2,1)} %copy.121) | data formatting | bytes 16777216 | tf_op jit(solution)/shard_map/reshape | solution.py:153
  493.6 23.8 %multiply_convert_fusion.3 = (bf16[16384,512]{1,0:T(8,128)(2,1)}, f32[16384,512]{1,0:T(8,128)}) fusion(f32[512]{0:T(512)S(1)} %copy-done.20, bf16[256,512]{1,0:T(8,128)(2,1)S(1)} %copy-done.6, f32[16384,256]{1,0:T(8,128)} %reshape.296, f32[256]{0:T(256)S(1)} %copy-done.13, f32[16384]{0:T(1024)S(1)} %rsqrt.12), kind=kOutput, calls=%fused_computation.6 | convolution fusion | flops 4357881856 | bytes 67439616 | tf_op jit(solution)/shard_map/dot_general | solution.py:57
  517.4 21.3 %fusion.51 = f32[16384,512]{1,0:T(8,128)} fusion(bf16[16384,512]{1,0:T(8,128)(2,1)} %get-tuple-element.65, bf16[512,512]{1,0:T(8,128)(2,1)S(1)} %copy-done), kind=kOutput, calls=%fused_computation.80 | convolution fusion | flops 8589934592 | bytes 50855936 | tf_op jit(solution)/shard_map/dot_general | solution.py:60
  538.7 26.0 %convert_reduce_fusion = (f32[512]{0:T(512)}, bf16[16384,512]{1,0:T(8,128)(2,1)}) fusion(f32[16384,512]{1,0:T(8,128)} %fusion.51, f32[512]{0:T(512)S(1)} %copy-done.21, bf16[16384,256]{1,0:T(8,128)(2,1)} %reshape.293, bf16[512,256]{1,0:T(8,128)(2,1)S(1)} %copy-done.19), kind=kOutput, calls=%fused_computation.1 | convolution fusion | flops 4395630080 | bytes 58986496 | tf_op jit(solution)/shard_map/dot_general | solution.py:46
  564.8 29.5 %convert_reduce_fusion.1 = (f32[512]{0:T(512)}, bf16[16384,512]{1,0:T(8,128)(2,1)}) fusion(f32[16384,512]{1,0:T(8,128)} %get-tuple-element.66, f32[512]{0:T(512)S(1)} %copy-done.20, bf16[16384,512]{1,0:T(8,128)(2,1)} %get-tuple-element.71, bf16[512,512]{1,0:T(8,128)(2,1)S(1)} %copy-done), kind=kOutput, calls=%fused_computation.2 | convolution fusion | flops 8690597888 | bytes 67637248 | tf_op jit(solution)/shard_map/dot_general | solution.py:46
  594.3 16.7 %fusion.49 = f32[256,512]{1,0:T(8,128)} fusion(bf16[16384,512]{1,0:T(8,128)(2,1)} %get-tuple-element.69, f32[16384,256]{1,0:T(8,128)} %reshape.296, f32[256]{0:T(256)S(1)} %copy-done.14, f32[16384]{0:T(1024)S(1)} %copy-done.5), kind=kOutput, calls=%fused_computation.78 | convolution fusion | flops 4307550208 | bytes 34145280 | tf_op jit(solution)/shard_map/dot_general | solution.py:40
  611.0 22.2 %multiply_reduce_fusion = (f32[256]{0:T(256)}, f32[16384]{0:T(1024)S(1)}, f32[16384,256]{1,0:T(8,128)}) fusion(f32[16384,256]{1,0:T(8,128)} %reshape.296, f32[16384]{0:T(1024)S(1)} %copy-done.5, f32[256]{0:T(256)S(1)} %copy-done.14, bf16[16384,512]{1,0:T(8,128)(2,1)} %get-tuple-element.69, bf16[256,512]{1,0:T(8,128)(2,1)S(1)} %copy-done.7), kind=kOutput, calls=%fused_computation.10 | convolution fusion | flops 4320116736 | bytes 50726912 | tf_op jit(solution)/shard_map/dot_general | solution.py:46
  633.3 17.1 %subtract_convert_fusion = bf16[16384,256]{1,0:T(8,128)(2,1)} fusion(f32[16384,256]{1,0:T(8,128)} %get-tuple-element.67, f32[16384,256]{1,0:T(8,128)} %reshape.296, f32[16384]{0:T(1024)S(1)} %broadcast_multiply_fusion.3, f32[256]{0:T(256)S(1)} %copy-done.14, f32[16384]{0:T(1024)S(1)} %copy-done.5), kind=kLoop, calls=%fused_computation.11 | loop fusion | flops 33554432 | bytes 42075136 | tf_op jit(solution)/shard_map/convert_element_type | solution.py:79
  650.4 12.6 %reshape.294 = bf16[512,8,4,256]{3,2,1,0:T(4,128)(2,1)} reshape(bf16[16384,256]{1,0:T(8,128)(2,1)} %subtract_convert_fusion) | data formatting | bytes 16777216 | tf_op jit(solution)/shard_map/reshape | solution.py:161
  662.9 16.5 %convert_bitcast_fusion = bf16[192,8,4,256,2]{3,0,4,2,1:T(8,128)(2,1)} fusion(bf16[512,8,4,256,1]{3,2,1,0,4:T(4,128)(2,1)} %bitcast.77, bf16[192,1,512]{2,0,1:T(8,128)(2,1)S(1)} %copy-done.11, bf16[192,1,512]{2,0,1:T(8,128)(2,1)S(1)} %copy-done.9), kind=kOutput, calls=%fused_computation.29 | convolution fusion | flops 3225157632 | bytes 15073280 | tf_op jit(solution)/shard_map/spo,otec->stecp/dot_general | solution.py:100
  679.4 14.1 %copy.124 = bf16[192,8,4,256,2]{0,1,4,3,2:T(8,128)(2,1)} copy(bf16[192,8,4,256,2]{3,0,4,2,1:T(8,128)(2,1)} %convert_bitcast_fusion) | data formatting | bytes 12582912 | tf_op jit(solution)/shard_map/convert_element_type | solution.py:102
  693.5 38.7 %reshape_reshape.11 = bf16[8,24,8,4,4,128]{1,0,2,5,4,3:T(8,128)(2,1)} reshape(bf16[192,8,4,256,2]{0,1,4,3,2:T(8,128)(2,1)} %copy.124) | data formatting | bytes 12582912 | tf_op jit(solution)/shard_map/reshape;reshape | solution.py:164
  732.2 44.6 %copy.125 = bf16[8,4,24,8,4,128]{5,3,4,2,1,0:T(8,128)(2,1)} copy(bf16[8,4,24,8,4,128]{2,0,3,5,1,4:T(8,128)(2,1)} %bitcast.73) | data formatting | bytes 12582912 | tf_op jit(solution)/shard_map/transpose | solution.py:165
  776.8 6.1 all-to-all-start.2
  782.9 0.0 copy-start.22
  782.9 0.0 all-reduce.4.cloned.1.call-start
  782.9 18.0 %fusion.52 = f32[512,512]{1,0:T(8,128)} fusion(bf16[16384,512]{1,0:T(8,128)(2,1)} %get-tuple-element.65, bf16[16384,512]{1,0:T(8,128)(2,1)} %get-tuple-element.71), kind=kOutput, calls=%fused_computation.81 | convolution fusion | flops 8589934592 | bytes 34603008 | tf_op jit(solution)/shard_map/dot_general | solution.py:40
  801.0 0.0 copy-start.18
  801.0 18.4 %fusion = f32[512,256]{1,0:T(8,128)} fusion(bf16[16384,256]{1,0:T(8,128)(2,1)} %reshape.293, f32[16384,512]{1,0:T(8,128)} %fusion.51, f32[512]{0:T(512)S(1)} %copy-done.22), kind=kOutput, calls=%fused_computation.15 | convolution fusion | flops 4345298944 | bytes 42469376 | tf_op jit(solution)/shard_map/dot_general | solution.py:40
  819.4 0.0 all-reduce.4.cloned.1.call-update
  819.5 136.3 %all-reduce = (f32[256]{0:T(256)S(1)}, f32[512]{0:T(512)S(1)}, f32[512]{0:T(512)S(1)}) all-reduce(f32[256]{0:T(256)S(1)} %copy-done.16, f32[512]{0:T(512)S(1)} %copy-done.18, f32[512]{0:T(512)S(1)} %copy-done.17), channel_id=1, replica_groups=mesh['lat'=8,'lev'=4] {'lat','lev'}, use_global_device_ids=true, to_apply=%region_3.4 | all-reduce | flops 1280 | bytes 10240 | tf_op jit(solution)/shard_map/psum | solution.py:168
  955.8 0.6 broadcast_multiply_fusion.7
  956.3 0.6 broadcast_multiply_fusion.5
  956.9 34.9 %all-reduce.4.cloned.1.call-done = (f32[256,512]{1,0:T(8,128)}, f32[512,512]{1,0:T(8,128)}, f32[512,256]{1,0:T(8,128)}) async-done(((f32[256,512]{1,0:T(8,128)}, f32[512,512]{1,0:T(8,128)}, f32[512,256]{1,0:T(8,128)}), (f32[256,512]{1,0:T(8,128)}, f32[512,512]{1,0:T(8,128)}, f32[512,256]{1,0:T(8,128)})) %all-reduce.4.cloned.1.call-update) | async-done | bytes 2097168 | tf_op jit(solution)/shard_map/psum | solution.py:168
  991.8 1.9 broadcast_multiply_fusion.2
  993.7 1.9 broadcast_multiply_fusion.1
  995.5 2.3 broadcast_multiply_fusion
  997.9 0.0 all-to-all-done.2
  997.9 7.3 fusion.1
  1005.2 10.1 copy.128
  (43 shorter events, 0.1 us)
Async XLA Ops:
  7.2 510.2 %copy-start = (bf16[512,512]{1,0:T(8,128)(2,1)S(1)}, bf16[512,512]{1,0:T(8,128)(2,1)}, u32[]{:S(2)}) copy-start(bf16[512,512]{1,0:T(8,128)(2,1)} %param.19) | copy-start | bytes 1572868
  11.0 26.3 %copy-start.2 = (bf16[24,171,256,1]{2,0,1,3:T(8,128)(2,1)}, bf16[24,171,256,1]{2,0,1,3:T(8,128)(2,1)S(1)}, u32[]{:S(2)}) copy-start(bf16[24,171,256,1]{2,0,1,3:T(8,128)(2,1)S(1)} %select_bitcast_fusion) | copy-start | bytes 6303748
  11.0 26.3 %copy-start.23 = (f32[256]{0:T(256)S(1)}, f32[256]{0:T(256)}, u32[]{:S(2)}) copy-start(f32[256]{0:T(256)} %param.14) | copy-start | bytes 3076
  28.9 147.4 %all-to-all-start = ((bf16[24,256,4,128]{3,2,0,1:T(4,128)(2,1)}), bf16[24,256,4,128]{3,2,0,1:T(4,128)(2,1)}, u32[]{:S(2)}, u32[]{:S(2)}) async-start(bf16[24,256,4,128]{3,2,0,1:T(4,128)(2,1)} %copy.108), calls=%async_computation | async-start | bytes 12582912 | tf_op jit(solution)/shard_map/all_to_all | solution.py:138
  37.2 143.0 %copy-start.15 = (s32[192]{0:T(256)S(1)}, s32[192]{0:T(256)}, u32[]{:S(2)}) copy-start(s32[192]{0:T(256)} %param.15) | copy-start | bytes 2308
  176.3 173.0 %all-to-all-start.1 = ((bf16[24,256,4,128]{3,2,0,1:T(4,128)(2,1)}), bf16[24,256,4,128]{3,2,0,1:T(4,128)(2,1)}, u32[]{:S(2)}, u32[]{:S(2)}) async-start(bf16[24,256,4,128]{3,2,0,1:T(4,128)(2,1)} %copy.116), calls=%async_computation.1 | async-start | bytes 12582912 | tf_op jit(solution)/shard_map/all_to_all | solution.py:139
  182.1 269.4 %copy-start.8 = (bf16[192,1,512]{2,0,1:T(8,128)(2,1)}, bf16[192,1,512]{2,0,1:T(8,128)(2,1)S(1)}, u32[]{:S(2)}) copy-start(bf16[192,1,512]{2,0,1:T(8,128)(2,1)S(1)} %get-tuple-element.61) | copy-start | bytes 589828
  182.1 269.4 %copy-start.10 = (bf16[192,1,512]{2,0,1:T(8,128)(2,1)}, bf16[192,1,512]{2,0,1:T(8,128)(2,1)S(1)}, u32[]{:S(2)}) copy-start(bf16[192,1,512]{2,0,1:T(8,128)(2,1)S(1)} %get-tuple-element.62) | copy-start | bytes 589828
  308.8 184.8 %copy-start.4 = (f32[16384]{0:T(1024)}, f32[16384]{0:T(1024)S(1)}, u32[]{:S(2)}) copy-start(f32[16384]{0:T(1024)S(1)} %rsqrt.12) | copy-start | bytes 196612
  468.7 24.9 %copy-start.6 = (bf16[256,512]{1,0:T(8,128)(2,1)S(1)}, bf16[256,512]{1,0:T(8,128)(2,1)}, u32[]{:S(2)}) copy-start(bf16[256,512]{1,0:T(8,128)(2,1)} %param.17) | copy-start | bytes 786436
  468.7 24.9 %copy-start.13 = (f32[256]{0:T(256)S(1)}, f32[256]{0:T(256)}, u32[]{:S(2)}) copy-start(f32[256]{0:T(256)} %param.16) | copy-start | bytes 3076
  468.7 24.9 %copy-start.20 = (f32[512]{0:T(512)S(1)}, f32[512]{0:T(512)}, u32[]{:S(2)}) copy-start(f32[512]{0:T(512)} %param.18) | copy-start | bytes 6148
  517.4 21.3 %copy-start.19 = (bf16[512,256]{1,0:T(8,128)(2,1)S(1)}, bf16[512,256]{1,0:T(8,128)(2,1)}, u32[]{:S(2)}) copy-start(bf16[512,256]{1,0:T(8,128)(2,1)} %param.21) | copy-start | bytes 786436
  517.4 21.3 %copy-start.21 = (f32[512]{0:T(512)S(1)}, f32[512]{0:T(512)}, u32[]{:S(2)}) copy-start(f32[512]{0:T(512)} %param.20) | copy-start | bytes 6148
  564.8 29.5 %copy-start.5 = (f32[16384]{0:T(1024)S(1)}, f32[16384]{0:T(1024)}, u32[]{:S(2)}) copy-start(f32[16384]{0:T(1024)} %copy-done.4) | copy-start | bytes 196612
  564.8 29.5 %copy-start.14 = (f32[256]{0:T(256)S(1)}, f32[256]{0:T(256)}, u32[]{:S(2)}) copy-start(f32[256]{0:T(256)} %param.16) | copy-start | bytes 3076
  594.3 16.7 %copy-start.7 = (bf16[256,512]{1,0:T(8,128)(2,1)S(1)}, bf16[256,512]{1,0:T(8,128)(2,1)}, u32[]{:S(2)}) copy-start(bf16[256,512]{1,0:T(8,128)(2,1)} %param.17) | copy-start | bytes 786436
  650.4 12.6 %copy-start.9 = (bf16[192,1,512]{2,0,1:T(8,128)(2,1)S(1)}, bf16[192,1,512]{2,0,1:T(8,128)(2,1)}, u32[]{:S(2)}) copy-start(bf16[192,1,512]{2,0,1:T(8,128)(2,1)} %copy-done.8) | copy-start | bytes 589828
  650.4 12.6 %copy-start.11 = (bf16[192,1,512]{2,0,1:T(8,128)(2,1)S(1)}, bf16[192,1,512]{2,0,1:T(8,128)(2,1)}, u32[]{:S(2)}) copy-start(bf16[192,1,512]{2,0,1:T(8,128)(2,1)} %copy-done.10) | copy-start | bytes 589828
  776.8 221.1 %all-to-all-start.2 = ((bf16[768,8,4,128]{3,1,2,0:T(8,128)(2,1)}), bf16[768,8,4,128]{3,1,2,0:T(8,128)(2,1)}, u32[]{:S(2)}, u32[]{:S(2)}) async-start(bf16[768,8,4,128]{3,1,2,0:T(8,128)(2,1)} %bitcast.74), calls=%async_computation.2 | async-start | bytes 12582912 | tf_op jit(solution)/shard_map/all_to_all | solution.py:167
  782.9 18.1 %copy-start.22 = (f32[512]{0:T(512)S(1)}, f32[512]{0:T(512)}, u32[]{:S(2)}) copy-start(f32[512]{0:T(512)} %param.20) | copy-start | bytes 6148
  782.9 208.9 %all-reduce.4.cloned.1.call-start = ((), (), s32[]{:S(2)}) async-start(), calls=%async_computation.3 | async-start | bytes 4194304 | tf_op jit(solution)/shard_map/psum | solution.py:168
  800.9 18.5 %copy-start.16 = (f32[256]{0:T(256)S(1)}, f32[256]{0:T(256)}, u32[]{:S(2)}) copy-start(f32[256]{0:T(256)} %get-tuple-element.49) | copy-start | bytes 3076
  800.9 18.5 %copy-start.17 = (f32[512]{0:T(512)S(1)}, f32[512]{0:T(512)}, u32[]{:S(2)}) copy-start(f32[512]{0:T(512)} %get-tuple-element.70) | copy-start | bytes 6148
  801.0 18.5 %copy-start.18 = (f32[512]{0:T(512)S(1)}, f32[512]{0:T(512)}, u32[]{:S(2)}) copy-start(f32[512]{0:T(512)} %get-tuple-element.68) | copy-start | bytes 6148
  801.0 196.9 %copy-start.3 = (bf16[24,171,256,1]{2,0,1,3:T(8,128)(2,1)S(1)}, bf16[24,171,256,1]{2,0,1,3:T(8,128)(2,1)}, u32[]{:S(2)}) copy-start(bf16[24,171,256,1]{2,0,1,3:T(8,128)(2,1)} %copy-done.2) | copy-start | bytes 6303748
  801.0 196.9 %copy-start.12 = (f32[24,171]{1,0:T(8,128)S(1)}, f32[24,171]{1,0:T(8,128)}, u32[]{:S(2)}) copy-start(f32[24,171]{1,0:T(8,128)} %get-tuple-element.60) | copy-start | bytes 49252
  997.9 17.4 %copy-start.1 = (bf16[512,512]{1,0:T(8,128)(2,1)S(1)}, bf16[512,512]{1,0:T(8,128)(2,1)}, u32[]{:S(2)}) copy-start(bf16[512,512]{1,0:T(8,128)(2,1)} %param.19) | copy-start | bytes 1572868
Sparse Core Ops, SparseCore 0:
  819.6 172.1 all-reduce.3
where the time goes:
time: 1030 us; the launch traced here: 1020 us
  local copies, waits for them, and re-layouts  413 us (40%)
  matrix products  253 us (25%)
  waiting for transfers between devices  157 us (15%)
  blocking collectives  136 us (13%)
  other arithmetic  30.6 us (3%)
  starting transfers between devices  17.6 us (2%)
  between operations  14.7 us (1%)
    psum x1, blocking collectives, local(): lax.psum((grads_local[0], grads_local[1], grads_local[2], grads_local[3],...  136 us
    all_to_all x1, waiting for transfers between devices, local(): lax.all_to_all(fourier, ('lat', 'lev'), split_axis=1, concat_axis=0, tile...  122 us
    transpose x2, local copies, waits for them, and re-layouts, regroup(): shaped = jnp.transpose(shaped, (0, 2, 3, 4, 1, 5))  111 us
    another operation x2, local copies, waits for them, and re-layouts, synthesize(): split = coeffs.reshape(shape[0], shape[1], shape[2], shape[3] // 2, 2)  78.1 us
    dot_general x3, matrix products, contract_cols(): lax.dot_general(left, right, (((1,), (1,)), ((), ())), preferred_element_...  77.8 us
    dot_general x3, matrix products, contract_rows(): lax.dot_general(left, right, (((0,), (0,)), ((), ())), preferred_element_...  53.2 us
    transpose x1, local copies, waits for them, and re-layouts, local(): shaped = jnp.transpose(shaped, (0, 4, 1, 2, 3, 5))  44.6 us
    convert_element_type x2, local copies, waits for them, and re-layouts, column_grads(): inputs = columns.astype(jnp.float32)  40.5 us
  transfers between devices with their start and end apart: 4, of which 2 were waited for; matrix products, arithmetic and copies ran while one was open for 23% of the time, Pallas kernels for 0%

commit v1 on v0

v1 whole, which is shorter than its diff:
```python
import functools
import math

import jax
import jax.numpy as jnp
from jax import lax
from jax.experimental import pallas as pl
from jax.experimental.pallas import tpu as pltpu
from jax.sharding import PartitionSpec as P

WAVES = 171
TIME_STEP = 0.5
NORM_EPS = 1e-06
NLON = 512
F32 = jnp.float32
BF16 = jnp.bfloat16


def fourier_table(waves_all):
    longitude = jnp.arange(NLON, dtype=jnp.int32)
    phase_steps = waves_all[:, None] * longitude[None, :] % NLON
    angles = phase_steps.astype(F32) * (2.0 * math.pi / NLON)
    weight_scale = jnp.where(waves_all < WAVES, math.sqrt(2.0 / NLON), 0.0).astype(F32)[:, None]
    return jnp.concatenate(
        [jnp.cos(angles) * weight_scale, -jnp.sin(angles) * weight_scale], axis=0
    ).astype(BF16)


def shrink_factor(degree_count):
    degree = jnp.arange(degree_count, dtype=jnp.int32)
    ratio = (degree * (degree + 1)).astype(F32) / float(WAVES * (WAVES - 1))
    return (1.0 / (1.0 + ratio * ratio))[:, None]


def split_parts(half):
    width = 2 * half
    src = lax.broadcasted_iota(jnp.int32, (width, width), 0)
    dst = lax.broadcasted_iota(jnp.int32, (width, width), 1)
    group, inner = src // half, src % half
    target = (inner % 2) * half + group * (half // 2) + inner // 2
    return (target == dst).astype(BF16)


def dot(left, right):
    return jnp.dot(left, right, preferred_element_type=F32)


def dot_rows(left, right):
    return lax.dot_general(left, right, (((0,), (0,)), ((), ())), preferred_element_type=F32)


def legendre_kernel(pair, members, degrees, is_cot, waves, x_ref, leg_ref, *rest):
    if is_cot:
        factor_ref, quad_ref, out_ref, wide = rest
    else:
        out_ref, wide = rest
    step = pl.program_id(0)
    wide[...] = x_ref[...].astype(F32)
    lat_count, _, _, rows, lanes = out_ref.shape
    for k in range(pair):
        m = waves[step * pair + k]
        degree = lax.broadcasted_iota(jnp.int32, leg_ref.shape[1:], 0)
        living = (degree >= m) & (m < WAVES)
        basis = jnp.where(living, leg_ref[k].astype(F32), 0.0).astype(BF16)
        parts = []
        for e in range(members):
            part = wide[pl.ds(k * degrees * members + e, degrees, stride=members), :]
            if is_cot:
                part = TIME_STEP * part * factor_ref[...]
            parts.append(part.astype(BF16))
        result = dot_rows(basis, jnp.concatenate(parts, axis=1))
        if is_cot:
            result = result * quad_ref[...]
        result = result.astype(BF16)
        for e in range(members):
            out_ref[:, e, k] = result[:, e * lanes : (e + 1) * lanes].reshape(lat_count, rows, lanes)


def legendre(waves, packed, legendre_table, chunk, chunks, lat_count, factor=None, quad=None):
    slots, degrees, nlat = legendre_table.shape
    lanes = packed.shape[1]
    members = packed.shape[0] // (slots * degrees)
    pair = 4 if slots % 4 == 0 else 2
    span = nlat // chunks
    rows = span // lat_count
    is_cot = factor is not None
    block = pair * degrees * members
    in_specs = [
        pl.BlockSpec((block, lanes), lambda i, w: (i, 0)),
        pl.BlockSpec((pair, degrees, span), lambda i, w: (i, 0, chunk)),
    ]
    operands = [packed, legendre_table]
    if is_cot:
        in_specs += [
            pl.BlockSpec((degrees, 1), lambda i, w: (0, 0)),
            pl.BlockSpec((span, 1), lambda i, w: (chunk, 0)),
        ]
        operands += [factor, quad]
    return pl.pallas_call(
        functools.partial(legendre_kernel, pair, members, degrees, is_cot),
        out_shape=jax.ShapeDtypeStruct((lat_count, members, slots, rows, lanes), BF16),
        grid_spec=pltpu.PrefetchScalarGridSpec(
            num_scalar_prefetch=1,
            grid=(slots // pair,),
            in_specs=in_specs,
            out_specs=pl.BlockSpec(
                (lat_count, members, pair, rows, lanes), lambda i, w: (0, 0, i, 0, 0)
            ),
            scratch_shapes=[pltpu.VMEM((block, lanes), F32)],
        ),
        compiler_params=pltpu.CompilerParams(
            dimension_semantics=("arbitrary",), vmem_limit_bytes=60 << 20
        ),
        cost_estimate=pl.CostEstimate(
            flops=2 * slots * degrees * span * members * lanes,
            bytes_accessed=2 * packed.size + 2 * slots * span * (degrees + members * lanes),
            transcendentals=0,
        ),
        name="legendre_cot" if is_cot else "legendre_state",
    )(waves, *operands)


def inverse_kernel(pair, members, degrees, chunks, waves, cot_ref, leg_ref, factor_ref, *rest):
    backs = rest[:chunks]
    out_ref, wide = rest[chunks:]
    step = pl.program_id(0)
    wide[...] = cot_ref[...].astype(F32)
    lat_count, _, _, rows, lanes = backs[0].shape
    for k in range(pair):
        m = waves[step * pair + k]
        degree = lax.broadcasted_iota(jnp.int32, leg_ref.shape[1:], 0)
        basis = jnp.where((degree >= m) & (m < WAVES), leg_ref[k].astype(F32), 0.0).astype(BF16)
        column = lax.broadcasted_iota(jnp.int32, (degrees, 1), 0)
        shrink = jnp.where((column >= m) & (m < WAVES), factor_ref[...], 0.0)
        sides = []
        for e in range(members):
            sides.append(
                jnp.concatenate(
                    [b[:, e, k].reshape(lat_count * rows, lanes) for b in backs], axis=0
                )
            )
        result = dot(basis, jnp.concatenate(sides, axis=1))
        for e in range(members):
            where = pl.ds(k * degrees * members + e, degrees, stride=members)
            out_ref[where, :] = wide[where, :] * shrink + result[:, e * lanes : (e + 1) * lanes]


def inverse_legendre(waves, packed, legendre_table, factor, backs):
    slots, degrees, nlat = legendre_table.shape
    lanes = packed.shape[1]
    members = packed.shape[0] // (slots * degrees)
    pair = 4 if slots % 4 == 0 else 2
    block = pair * degrees * members
    lat_count, _, _, rows, _ = backs[0].shape
    chunks = len(backs)
    return pl.pallas_call(
        functools.partial(inverse_kernel, pair, members, degrees, chunks),
        out_shape=jax.ShapeDtypeStruct(packed.shape, F32),
        grid_spec=pltpu.PrefetchScalarGridSpec(
            num_scalar_prefetch=1,
            grid=(slots // pair,),
            in_specs=[
                pl.BlockSpec((block, lanes), lambda i, w: (i, 0)),
                pl.BlockSpec((pair, degrees, nlat), lambda i, w: (i, 0, 0)),
                pl.BlockSpec((degrees, 1), lambda i, w: (0, 0)),
            ]
            + [
                pl.BlockSpec((lat_count, members, pair, rows, lanes), lambda i, w: (0, 0, i, 0, 0))
            ]
            * chunks,
            out_specs=pl.BlockSpec((block, lanes), lambda i, w: (i, 0)),
            scratch_shapes=[pltpu.VMEM((block, lanes), F32)],
        ),
        compiler_params=pltpu.CompilerParams(
            dimension_semantics=("arbitrary",), vmem_limit_bytes=60 << 20
        ),
        cost_estimate=pl.CostEstimate(
            flops=2 * slots * degrees * nlat * members * lanes,
            bytes_accessed=6 * packed.size + 2 * slots * nlat * (degrees + members * lanes),
            transcendentals=0,
        ),
        name="inverse_legendre",
    )(waves, packed, legendre_table, factor, *backs)


def sigmoid(z):
    return 0.5 + 0.5 * jnp.tanh(0.5 * z)


def column_kernel(
    rows,
    block,
    state_ref,
    cot_ref,
    table_ref,
    back_table_ref,
    split_ref,
    merge_ref,
    gain_ref,
    w_in_ref,
    b_in_ref,
    w_mid_ref,
    b_mid_ref,
    w_in_t_ref,
    w_mid_t_ref,
    w_out_t_ref,
    out_ref,
    grad_ref,
    state_wide,
    cot_wide,
    out_wide,
    state_mat,
    cot_mat,
    back_acc,
):
    row, part = pl.program_id(0), pl.program_id(1)
    last_part = pl.num_programs(1) - 1
    lat_count, groups, slots_here, _, lanes = state_ref.shape
    slots = lat_count * slots_here
    hidden = w_in_ref.shape[1]
    channels = w_in_ref.shape[0]

    @pl.when((row == 0) & (part == 0))
    def _():
        grad_ref[...] = jnp.zeros_like(grad_ref)

        @pl.loop(0, lat_count)
        def _(i):
            size = slots_here * rows
            for j in range(groups):
                where = pl.ds(pl.multiple_of(i * size, 8), size)
                state_wide[j, where, :] = state_ref[i, j].astype(F32).reshape(size, lanes)
                cot_wide[j, where, :] = cot_ref[i, j].astype(F32).reshape(size, lanes)

    @pl.when(part == 0)
    def _():
        for wide, mat in ((state_wide, state_mat), (cot_wide, cot_mat)):
            for q in range(groups // 2):
                both = jnp.concatenate(
                    [wide[2 * q + j, pl.ds(row, slots, stride=rows), :].astype(BF16) for j in (0, 1)],
                    axis=1,
                )
                apart = dot(both, split_ref[...]).astype(BF16)
                for p in (0, 1):
                    mat[p * slots : (p + 1) * slots, q * lanes : (q + 1) * lanes] = apart[
                        :, p * lanes : (p + 1) * lanes
                    ]

    table = table_ref[pl.ds(pl.multiple_of(part * block, block), block), :]
    values = dot(table, state_mat[...]).astype(BF16).astype(F32)
    cot = dot(table, cot_mat[...]).astype(BF16)
    gain = gain_ref[...]
    inverse = lax.rsqrt(jnp.mean(values * values, axis=1, keepdims=True) + NORM_EPS)
    unit = values * inverse
    normed = (unit * gain).astype(BF16)
    pre_one = dot(normed, w_in_ref[...]) + b_in_ref[...]
    sig_one = sigmoid(pre_one)
    soft_one = pre_one * sig_one
    slope_one = sig_one + soft_one * (1.0 - sig_one)
    act_one = soft_one.astype(BF16)
    pre_two = dot(act_one, w_mid_ref[...]) + b_mid_ref[...]
    sig_two = sigmoid(pre_two)
    soft_two = pre_two * sig_two
    slope_two = sig_two + soft_two * (1.0 - sig_two)
    act_two = soft_two.astype(BF16)
    delta_two = (dot(cot, w_out_t_ref[...]) * slope_two).astype(BF16)
    delta_one = (dot(delta_two, w_mid_t_ref[...]) * slope_one).astype(BF16)
    back_norm = dot(delta_one, w_in_t_ref[...])
    grad_ref[:channels, :] += dot_rows(normed, delta_one)
    grad_ref[channels : channels + hidden, :] += dot_rows(act_one, delta_two)
    base = channels + hidden
    grad_ref[base : base + channels, :] += dot_rows(cot, act_two)
    base += channels
    grad_ref[base : base + 1, :] += jnp.sum(delta_one.astype(F32), axis=0, keepdims=True)
    grad_ref[base + 1 : base + 2, :] += jnp.sum(delta_two.astype(F32), axis=0, keepdims=True)
    grad_ref[base + 2 : base + 3, :channels] += jnp.sum(back_norm * unit, axis=0, keepdims=True)
    scaled = back_norm * gain
    mean = jnp.mean(scaled * values, axis=1, keepdims=True)
    grad_columns = (inverse * scaled - values * (inverse * inverse * inverse) * mean).astype(BF16)
    back = dot(back_table_ref[:, pl.ds(pl.multiple_of(part * block, block), block)], grad_columns)

    @pl.when(part == 0)
    def _():
        back_acc[...] = back

    @pl.when(part > 0)
    def _():
        back_acc[...] += back

    @pl.when(part == last_part)
    def _():
        for q in range(groups // 2):
            apart = jnp.concatenate(
                [
                    back_acc[p * slots : (p + 1) * slots, q * lanes : (q + 1) * lanes].astype(BF16)
                    for p in (0, 1)
                ],
                axis=1,
            )
            both = dot(apart, merge_ref[...])
            for j in (0, 1):
                out_wide[2 * q + j, pl.ds(row, slots, stride=rows), :] = both[
                    :, j * lanes : (j + 1) * lanes
                ]

    @pl.when((row == rows - 1) & (part == last_part))
    def _():
        @pl.loop(0, lat_count)
        def _(i):
            size = slots_here * rows
            for j in range(groups):
                where = pl.ds(pl.multiple_of(i * size, 8), size)
                out_ref[i, j] = out_wide[j, where, :].astype(BF16).reshape(slots_here, rows, lanes)


def column_grads(state, cot, table, back_table, split, merge, gain, weights):
    lat_count, groups, slots_here, rows, lanes = state.shape
    slots = lat_count * slots_here
    weight_in, bias_in, weight_mid, bias_mid, weight_out = weights
    channels, hidden = weight_in.shape
    block = NLON // 2
    grad_rows = 2 * channels + hidden + 8
    operands = [
        state,
        cot,
        table,
        back_table,
        split,
        merge,
        gain,
        weight_in,
        bias_in[None, :],
        weight_mid,
        bias_mid[None, :],
        weight_in.T,
        weight_mid.T,
        weight_out.T,
    ]

    def whole(shape):
        return pl.BlockSpec(shape, lambda i, j: (0,) * len(shape), pipeline_mode=pl.Buffered(1))

    out_shapes = (
        jax.ShapeDtypeStruct(state.shape, BF16),
        jax.ShapeDtypeStruct((grad_rows, hidden), F32),
    )
    wide = pltpu.VMEM((groups, slots * rows, lanes), F32)
    mat = pltpu.VMEM((2 * slots, channels), BF16)
    per_column = channels * hidden * 6 + hidden * hidden * 3 + 6 * slots * channels
    return pl.pallas_call(
        functools.partial(column_kernel, rows, block),
        out_shape=out_shapes,
        grid=(rows, NLON // block),
        in_specs=[whole(o.shape) for o in operands],
        out_specs=tuple(whole(o.shape) for o in out_shapes),
        scratch_shapes=[wide, wide, wide, mat, mat, pltpu.VMEM((2 * slots, channels), F32)],
        compiler_params=pltpu.CompilerParams(
            dimension_semantics=("arbitrary", "arbitrary"), vmem_limit_bytes=60 << 20
        ),
        cost_estimate=pl.CostEstimate(
            flops=2 * rows * NLON * per_column,
            bytes_accessed=6 * state.size + 4 * grad_rows * hidden,
            transcendentals=2 * rows * NLON * hidden,
        ),
        name="columns",
    )(*operands)


def local(
    spec_in,
    cotangent,
    legendre_table,
    quad_weights,
    wave_order,
    norm_gain,
    weight_in,
    bias_in,
    weight_mid,
    bias_mid,
    weight_out,
):
    axes = ("lat", "lev")
    slots_here, degrees, members, lanes = spec_in.shape
    nlat = legendre_table.shape[2]
    lat_count = lax.axis_size("lat")
    lev_count = lax.axis_size("lev")
    assert members == lev_count
    chunks = 2 if nlat // lat_count >= 16 else 1
    own_waves = lax.dynamic_slice_in_dim(wave_order, lax.axis_index("lat") * slots_here, slots_here)
    factor = shrink_factor(degrees)
    quad = quad_weights[:, None]
    spec_rows = spec_in.reshape(slots_here * degrees * members, lanes)
    cot_rows = cotangent.reshape(slots_here * degrees * members, lanes)
    count = lat_count * lev_count

    def exchange(x):
        shape = x.shape
        x = x.reshape((count,) + shape[2:])
        x = lax.all_to_all(x, axes, split_axis=0, concat_axis=0, tiled=True)
        return x.reshape(shape)

    table = fourier_table(wave_order)
    split = split_parts(lanes)
    received, before = [], None
    for k in range(chunks):
        state = legendre(own_waves, spec_rows, legendre_table, k, chunks, lat_count)
        if before is not None:
            state, before = lax.optimization_barrier((state, before))
            received[-1] = (received[-1][0], before)
        state = exchange(state)
        cot = legendre(own_waves, cot_rows, legendre_table, k, chunks, lat_count, factor, quad)
        cot, state = lax.optimization_barrier((cot, state))
        cot = before = exchange(cot)
        received.append((state, cot))
    weights = (weight_in, bias_in, weight_mid, bias_mid, weight_out)
    backs, totals = [], []
    for state, cot in received:
        back, grads = column_grads(
            state, cot, table.T, table, split, split.T, norm_gain[None, :], weights
        )
        backs.append(exchange(back))
        totals.append(grads)
    summed = lax.psum(functools.reduce(jnp.add, totals), axes)
    channels, hidden = weight_in.shape
    summed = summed * float(members * nlat * NLON) ** (-0.5)
    base = 2 * channels + hidden
    grad_w_in = summed[:channels]
    grad_w_mid = summed[channels : channels + hidden]
    grad_w_out = summed[channels + hidden : base].T
    grad_spec = inverse_legendre(own_waves, cot_rows, legendre_table, factor, backs)
    return (
        grad_spec.reshape(spec_in.shape),
        summed[base + 2, :channels],
        grad_w_in,
        summed[base],
        grad_w_mid,
        summed[base + 1],
        grad_w_out,
    )


def solution(mesh):
    placed = (
        P("lat", None, None, "lev"),
        P("lat", None, None, "lev"),
        P("lat", None, None),
    ) + (P(),) * 8
    return jax.shard_map(
        local,
        mesh=mesh,
        in_specs=placed,
        out_specs=(P("lat", None, None, "lev"),) + (P(),) * 6,
        check_vma=False,
    )
```

time: 1030 us -> 618 us (0.60)
  local copies, waits for them, and re-layouts: 413 us -> 17.5 us
  matrix products: 253 us -> 0 us
  waiting for transfers between devices: 157 us -> 352 us
  Pallas kernels: 0 us -> 192 us
  blocking collectives: 136 us -> 0 us
  other arithmetic: 30.6 us -> 10.3 us
  starting transfers between devices: 17.6 us -> 31.4 us
    dot_general x14 -> x0, matrix products: 253 us -> none  [the longest x3 77.8 us: contract_cols(): lax.dot_general(left, right, (((1,), (1,)), ((), ())), preferred_element_...]
    pallas_call x0 -> x7, Pallas kernels: none -> 192 us  [the longest x2 151 us: column_grads(): pl.pallas_call(functools.partial(column_kernel, rows, block), out_shape=o...]
    transpose x3 -> x2, local copies, waits for them, and re-layouts: 155 us -> 1.78 us  [the longest x1 0.92 us: local(): back, grads = column_grads(state, cot, table.T, table, split, split.T, no...]
    psum x1 -> x0, blocking collectives: 136 us -> none  [local(): lax.psum((grads_local[0], grads_local[1], grads_local[2], grads_local[3],...]
    psum x1, waiting for transfers between devices: 34.9 us -> 162 us  [local(): summed = lax.psum(functools.reduce(jnp.add, totals), axes)]
    another operation x3 -> x0, local copies, waits for them, and re-layouts: 117 us -> none  [the longest x2 78.1 us: synthesize(): split = coeffs.reshape(shape[0], shape[1], shape[2], shape[3] // 2, 2)]
    convert_element_type x6 -> x0, local copies, waits for them, and re-layouts: 87.5 us -> none  [the longest x2 40.5 us: column_grads(): inputs = columns.astype(jnp.float32)]
    all_to_all x3 -> x6, waiting for transfers between devices: 122 us -> 190 us  [exchange(): x = lax.all_to_all(x, axes, split_axis=0, concat_axis=0, tiled=True)]
  transfers between devices with their start and end apart: 4 -> 7, of which waited for: 2 -> 4; matrix products, arithmetic and copies ran while one was open for 23% -> 3% of each run, Pallas kernels for 0% -> 28%
where the time goes in v1:
time: 618 us; the launch traced here: 617 us
  waiting for transfers between devices  352 us (57%)
  Pallas kernels  192 us (31%)
  starting transfers between devices  31.4 us (5%)
  local copies, waits for them, and re-layouts  17.5 us (3%)
  between operations  14.2 us (2%)
  other arithmetic  10.3 us (2%)
    all_to_all x6, waiting for transfers between devices, exchange(): x = lax.all_to_all(x, axes, split_axis=0, concat_axis=0, tiled=True)  190 us
    psum x1, waiting for transfers between devices, local(): summed = lax.psum(functools.reduce(jnp.add, totals), axes)  162 us
    pallas_call x2, Pallas kernels, column_grads(): pl.pallas_call(functools.partial(column_kernel, rows, block), out_shape=o...  151 us
    all_to_all x6, starting transfers between devices, exchange(): x = lax.all_to_all(x, axes, split_axis=0, concat_axis=0, tiled=True)  31.4 us
    pallas_call x4, Pallas kernels, legendre(): pl.pallas_call(functools.partial(legendre_kernel, pair, members, degrees,...  29.7 us
  transfers between devices with their start and end apart: 7, of which 4 were waited for; matrix products, arithmetic and copies ran while one was open for 3% of the time, Pallas kernels for 28%

profile of v1, /device:TPU:0, one launch (start us, length us, event | category | flops | bytes accessed | tf_op | source)
XLA Modules:
  0.0 616.8 jit_solution(13691840016934574260)
XLA Ops:
  7.2 0.0 copy-start.6
  7.2 3.4 copy.55.leg_ref
  10.6 0.0 copy-done.6
  10.6 0.6 dynamic_slice.3.waves
  11.2 7.2 %legendre_state.2 = bf16[8,4,24,16,128]{4,3,2,1,0:T(8,128)(2,1)} custom-call(s32[24]{0:T(128)} %dynamic_slice.3.waves, bf16[16416,128]{1,0:T(8,128)(2,1)} %bitcast.32, bf16[24,171,256]{2,1,0:T(8,128)(2,1)} %copy.55.leg_ref), custom_call_target="tpu_custom_call" | custom-call | flops 537919488 | bytes 8398848 | tf_op jit(solution)/shard_map/legendre_state/pallas_call | solution.py:99
  18.4 0.0 copy-start.7
  18.4 7.3 %all-to-all-start = ((bf16[32,24,16,128]{3,2,1,0:T(8,128)(2,1)}), bf16[32,24,16,128]{3,2,1,0:T(8,128)(2,1)S(1)}, u32[]{:S(2)}, u32[]{:S(2)}) async-start(bf16[32,24,16,128]{3,2,1,0:T(8,128)(2,1)} %bitcast.37), calls=%async_computation | async-start | bytes 6291456 | tf_op jit(solution)/shard_map/all_to_all | solution.py:399
  25.7 0.0 copy-done.7
  25.7 0.8 copy.45.rest_1_
  26.5 0.7 fusion.28.rest_0_.factor_ref
  27.2 7.7 %legendre_cot.2 = bf16[8,4,24,16,128]{4,3,2,1,0:T(8,128)(2,1)} custom-call(s32[24]{0:T(128)} %dynamic_slice.3.waves, bf16[16416,128]{1,0:T(8,128)(2,1)} %bitcast.29, bf16[24,171,256]{2,1,0:T(8,128)(2,1)} %copy.55.leg_ref, f32[171,1]{1,0:T(8,128)} %fusion.28.rest_0_.factor_ref, f32[256,1]{1,0:T(8,128)} %copy.45.rest_1_), custom_call_target="tpu_custom_call" | custom-call | flops 537919488 | bytes 8398848 | tf_op jit(solution)/shard_map/legendre_cot/pallas_call | solution.py:99
  34.9 62.2 %all-to-all-done = bf16[32,24,16,128]{3,2,1,0:T(8,128)(2,1)S(1)} async-done(((bf16[32,24,16,128]{3,2,1,0:T(8,128)(2,1)}), bf16[32,24,16,128]{3,2,1,0:T(8,128)(2,1)S(1)}, u32[]{:S(2)}, u32[]{:S(2)}) %all-to-all-start) | async-done | bytes 3145760 | tf_op jit(solution)/shard_map/all_to_all | solution.py:399
  97.0 0.0 copy-start.1
  97.0 1.7 copy-done.1
  98.7 4.1 all-to-all-start.1
  102.9 7.3 %legendre_state.3 = bf16[8,4,24,16,128]{4,3,2,1,0:T(8,128)(2,1)} custom-call(s32[24]{0:T(128)} %dynamic_slice.3.waves, bf16[16416,128]{1,0:T(8,128)(2,1)} %bitcast.33, bf16[24,171,256]{2,1,0:T(8,128)(2,1)} %copy.55.leg_ref), custom_call_target="tpu_custom_call" | custom-call | flops 537919488 | bytes 8398848 | tf_op jit(solution)/shard_map/legendre_state/pallas_call | solution.py:99
  110.1 64.0 %all-to-all-done.1 = bf16[32,24,16,128]{3,2,1,0:T(8,128)(2,1)} async-done(((bf16[32,24,16,128]{3,2,1,0:T(8,128)(2,1)}), bf16[32,24,16,128]{3,2,1,0:T(8,128)(2,1)}, u32[]{:S(2)}, u32[]{:S(2)}) %all-to-all-start.1) | async-done | bytes 3145760 | tf_op jit(solution)/shard_map/all_to_all | solution.py:399
  174.2 4.0 all-to-all-start.3
  178.2 7.6 %legendre_cot.3 = bf16[8,4,24,16,128]{4,3,2,1,0:T(8,128)(2,1)} custom-call(s32[24]{0:T(128)} %dynamic_slice.3.waves, bf16[16416,128]{1,0:T(8,128)(2,1)} %bitcast.30, bf16[24,171,256]{2,1,0:T(8,128)(2,1)} %copy.55.leg_ref, f32[171,1]{1,0:T(8,128)} %fusion.28.rest_0_.factor_ref, f32[256,1]{1,0:T(8,128)} %copy.45.rest_1_), custom_call_target="tpu_custom_call" | custom-call | flops 537919488 | bytes 8398848 | tf_op jit(solution)/shard_map/legendre_cot/pallas_call | solution.py:99
  185.8 63.7 %all-to-all-done.3 = bf16[32,24,16,128]{3,2,1,0:T(8,128)(2,1)S(1)} async-done(((bf16[32,24,16,128]{3,2,1,0:T(8,128)(2,1)}), bf16[32,24,16,128]{3,2,1,0:T(8,128)(2,1)S(1)}, u32[]{:S(2)}, u32[]{:S(2)}) %all-to-all-start.3) | async-done | bytes 3145760 | tf_op jit(solution)/shard_map/all_to_all | solution.py:399
  249.5 0.0 copy-start.2
  249.5 0.0 copy-start.5
  249.5 1.7 copy-done.2
  251.2 4.1 all-to-all-start.4
  255.4 0.0 copy-start.3
  255.4 0.0 copy-start.4
  255.4 1.9 multiply_convert_fusion.1
  257.3 0.8 pad_maximum_fusion
  258.1 0.9 copy.51.table_ref
  259.0 0.0 copy-done.5
  259.0 0.8 copy.48
  259.9 0.0 copy-done.3
  259.9 1.0 copy.49
  260.9 0.0 copy-done.4
  260.9 0.8 copy.50
  261.8 1.0 fusion.22
  262.7 75.7 %columns.2 = (bf16[8,4,24,16,128]{4,3,2,1,0:T(8,128)(2,1)}, f32[1032,512]{1,0:T(8,128)}) custom-call(bf16[8,4,24,16,128]{4,3,2,1,0:T(8,128)(2,1)} %bitcast.40, bf16[8,4,24,16,128]{4,3,2,1,0:T(8,128)(2,1)} %bitcast.6.cot_ref, bf16[512,384]{1,0:T(8,128)(2,1)} %copy.51.table_ref, bf16[384,512]{1,0:T(8,128)(2,1)} %get-tuple-element.52.back_table_ref, ...), custom_call_target="tpu_custom_call" | custom-call | flops 30601641984 | bytes 11550720 | tf_op jit(solution)/shard_map/columns/pallas_call | solution.py:350
  338.5 0.0 all-to-all-done.4
  338.5 5.8 all-to-all-start.2
  344.2 75.7 %columns.3 = (bf16[8,4,24,16,128]{4,3,2,1,0:T(8,128)(2,1)}, f32[1032,512]{1,0:T(8,128)}) custom-call(bf16[8,4,24,16,128]{4,3,2,1,0:T(8,128)(2,1)} %bitcast.41, bf16[8,4,24,16,128]{4,3,2,1,0:T(8,128)(2,1)} %bitcast.19.cot_ref, bf16[512,384]{1,0:T(8,128)(2,1)} %copy.51.table_ref, bf16[384,512]{1,0:T(8,128)(2,1)} %get-tuple-element.52.back_table_ref, ...), custom_call_target="tpu_custom_call" | custom-call | flops 30601641984 | bytes 11550720 | tf_op jit(solution)/shard_map/columns/pallas_call | solution.py:350
  420.0 0.0 all-to-all-done.2
  420.0 0.0 copy-start
  420.0 1.7 copy-done
  421.6 5.9 all-to-all-start.5
  427.6 0.0 all-reduce.2.cloned.1.call-start
  427.7 4.1 add.105
  431.8 0.0 all-reduce.2.cloned.1.call-update
  431.8 161.7 %all-reduce.2.cloned.1.call-done = f32[1032,512]{1,0:T(8,128)} async-done(((f32[1032,512]{1,0:T(8,128)}), f32[1032,512]{1,0:T(8,128)}) %all-reduce.2.cloned.1.call-update) | async-done | bytes 2113552 | tf_op jit(solution)/shard_map/psum | solution.py:423
  593.5 1.8 broadcast_multiply_fusion
  595.4 0.6 slice.24
  595.9 1.0 slice.27
  597.0 0.9 slice_bitcast_fusion
  597.8 1.0 copy.56
  598.8 0.6 fusion.32
  599.4 0.0 all-to-all-done.5
  599.4 10.5 %inverse_legendre.1 = f32[16416,128]{1,0:T(8,128)} custom-call(s32[24]{0:T(128)} %dynamic_slice.3.waves, bf16[16416,128]{1,0:T(8,128)(2,1)} %bitcast.31, bf16[24,171,256]{2,1,0:T(8,128)(2,1)} %copy.55.leg_ref, f32[171,1]{1,0:T(8,128)} %fusion.28.rest_0_.factor_ref, bf16[8,4,24,16,128]{4,3,2,1,0:T(8,128)(2,1)} %bitcast.38, ...), custom_call_target="tpu_custom_call" | custom-call | flops 1075838976 | bytes 21000192 | tf_op jit(solution)/shard_map/inverse_legendre/pallas_call | solution.py:156
  (4 shorter events, 0.0 us)
Async XLA Ops:
  7.2 3.4 copy-start.6
  18.4 7.3 %copy-start.7 = (f32[256]{0:T(256)S(1)}, f32[256]{0:T(256)}, u32[]{:S(2)}) copy-start(f32[256]{0:T(256)} %param.14) | copy-start | bytes 3076
  18.4 78.7 %all-to-all-start = ((bf16[32,24,16,128]{3,2,1,0:T(8,128)(2,1)}), bf16[32,24,16,128]{3,2,1,0:T(8,128)(2,1)S(1)}, u32[]{:S(2)}, u32[]{:S(2)}) async-start(bf16[32,24,16,128]{3,2,1,0:T(8,128)(2,1)} %bitcast.37), calls=%async_computation | async-start | bytes 6291456 | tf_op jit(solution)/shard_map/all_to_all | solution.py:399
  97.0 1.7 copy-start.1
  98.7 75.5 %all-to-all-start.1 = ((bf16[32,24,16,128]{3,2,1,0:T(8,128)(2,1)}), bf16[32,24,16,128]{3,2,1,0:T(8,128)(2,1)}, u32[]{:S(2)}, u32[]{:S(2)}) async-start(bf16[32,24,16,128]{3,2,1,0:T(8,128)(2,1)} %bitcast.35), calls=%async_computation.1 | async-start | bytes 6291456 | tf_op jit(solution)/shard_map/all_to_all | solution.py:399
  174.2 75.4 %all-to-all-start.3 = ((bf16[32,24,16,128]{3,2,1,0:T(8,128)(2,1)}), bf16[32,24,16,128]{3,2,1,0:T(8,128)(2,1)S(1)}, u32[]{:S(2)}, u32[]{:S(2)}) async-start(bf16[32,24,16,128]{3,2,1,0:T(8,128)(2,1)} %bitcast.36), calls=%async_computation.3 | async-start | bytes 6291456 | tf_op jit(solution)/shard_map/all_to_all | solution.py:399
  249.5 1.7 copy-start.2
  249.5 9.5 %copy-start.5 = (bf16[256,512]{1,0:T(8,128)(2,1)S(1)}, bf16[256,512]{1,0:T(8,128)(2,1)}, u32[]{:S(2)}) copy-start(bf16[256,512]{1,0:T(8,128)(2,1)} %w_in_ref.3) | copy-start | bytes 786436
  251.2 87.2 %all-to-all-start.4 = ((bf16[32,24,16,128]{3,2,1,0:T(8,128)(2,1)}), bf16[32,24,16,128]{3,2,1,0:T(8,128)(2,1)}, u32[]{:S(2)}, u32[]{:S(2)}) async-start(bf16[32,24,16,128]{3,2,1,0:T(8,128)(2,1)} %bitcast.34), calls=%async_computation.4 | async-start | bytes 6291456 | tf_op jit(solution)/shard_map/all_to_all | solution.py:399
  255.4 4.5 copy-start.3
  255.4 5.5 copy-start.4
  338.5 81.5 %all-to-all-start.2 = ((bf16[32,24,16,128]{3,2,1,0:T(8,128)(2,1)}), bf16[32,24,16,128]{3,2,1,0:T(8,128)(2,1)S(1)}, u32[]{:S(2)}, u32[]{:S(2)}) async-start(bf16[32,24,16,128]{3,2,1,0:T(8,128)(2,1)} %bitcast.43), calls=%async_computation.2 | async-start | bytes 6291456 | tf_op jit(solution)/shard_map/all_to_all | solution.py:399
  420.0 1.7 copy-start
  421.6 177.8 %all-to-all-start.5 = ((bf16[32,24,16,128]{3,2,1,0:T(8,128)(2,1)}), bf16[32,24,16,128]{3,2,1,0:T(8,128)(2,1)}, u32[]{:S(2)}, u32[]{:S(2)}) async-start(bf16[32,24,16,128]{3,2,1,0:T(8,128)(2,1)} %bitcast.42), calls=%async_computation.5 | async-start | bytes 6291456 | tf_op jit(solution)/shard_map/all_to_all | solution.py:399
  427.6 165.9 %all-reduce.2.cloned.1.call-start = ((), (), s32[]{:S(2)}) async-start(), calls=%async_computation.6 | async-start | bytes 4227072 | tf_op jit(solution)/shard_map/psum | solution.py:423
Sparse Core Ops, SparseCore 0:
  434.0 159.4 all-reduce.1

commit v2 on v1

--- a/solution.py
+++ b/solution.py
@@ -120,9 +120,8 @@
     )(waves, *operands)
 
 
-def inverse_kernel(pair, members, degrees, chunks, waves, cot_ref, leg_ref, factor_ref, *rest):
-    backs = rest[:chunks]
-    out_ref, wide = rest[chunks:]
+def inverse_kernel(pair, members, degrees, subs, waves, cot_ref, leg_ref, factor_ref, *rest):
+    *backs, out_ref, wide = rest
     step = pl.program_id(0)
     wide[...] = cot_ref[...].astype(F32)
     lat_count, _, _, rows, lanes = backs[0].shape
@@ -134,18 +133,19 @@
         shrink = jnp.where((column >= m) & (m < WAVES), factor_ref[...], 0.0)
         sides = []
         for e in range(members):
-            sides.append(
-                jnp.concatenate(
-                    [b[:, e, k].reshape(lat_count * rows, lanes) for b in backs], axis=0
-                )
-            )
+            pieces = []
+            for first in range(0, len(backs), subs):
+                subrows = [b[:, e, k].astype(F32) for b in backs[first : first + subs]]
+                joined = jnp.concatenate(subrows, axis=1)
+                pieces.append(joined.reshape(lat_count * subs * rows, lanes))
+            sides.append(jnp.concatenate(pieces, axis=0).astype(BF16))
         result = dot(basis, jnp.concatenate(sides, axis=1))
         for e in range(members):
             where = pl.ds(k * degrees * members + e, degrees, stride=members)
             out_ref[where, :] = wide[where, :] * shrink + result[:, e * lanes : (e + 1) * lanes]
 
 
-def inverse_legendre(waves, packed, legendre_table, factor, backs):
+def inverse_legendre(waves, packed, legendre_table, factor, backs, subs):
     slots, degrees, nlat = legendre_table.shape
     lanes = packed.shape[1]
     members = packed.shape[0] // (slots * degrees)
@@ -154,7 +154,7 @@
     lat_count, _, _, rows, _ = backs[0].shape
     chunks = len(backs)
     return pl.pallas_call(
-        functools.partial(inverse_kernel, pair, members, degrees, chunks),
+        functools.partial(inverse_kernel, pair, members, degrees, subs),
         out_shape=jax.ShapeDtypeStruct(packed.shape, F32),
         grid_spec=pltpu.PrefetchScalarGridSpec(
             num_scalar_prefetch=1,
@@ -190,6 +190,7 @@
 def column_kernel(
     rows,
     block,
+    chained,
     state_ref,
     cot_ref,
     table_ref,
@@ -204,15 +205,11 @@
     w_in_t_ref,
     w_mid_t_ref,
     w_out_t_ref,
-    out_ref,
-    grad_ref,
-    state_wide,
-    cot_wide,
-    out_wide,
-    state_mat,
-    cot_mat,
-    back_acc,
+    *rest,
 ):
+    if chained:
+        before_ref, *rest = rest
+    out_ref, grad_ref, state_wide, cot_wide, out_wide, state_mat, cot_mat, back_acc = rest
     row, part = pl.program_id(0), pl.program_id(1)
     last_part = pl.num_programs(1) - 1
     lat_count, groups, slots_here, _, lanes = state_ref.shape
@@ -222,7 +219,7 @@
 
     @pl.when((row == 0) & (part == 0))
     def _():
-        grad_ref[...] = jnp.zeros_like(grad_ref)
+        grad_ref[...] = before_ref[...] if chained else jnp.zeros_like(grad_ref)
 
         @pl.loop(0, lat_count)
         def _(i):
@@ -313,16 +310,14 @@
                 out_ref[i, j] = out_wide[j, where, :].astype(BF16).reshape(slots_here, rows, lanes)
 
 
-def column_grads(state, cot, table, back_table, split, merge, gain, weights):
-    lat_count, groups, slots_here, rows, lanes = state.shape
+def column_grads(state, cot, sub, rows, table, back_table, split, merge, gain, weights, before):
+    lat_count, groups, slots_here, _, lanes = state.shape
     slots = lat_count * slots_here
     weight_in, bias_in, weight_mid, bias_mid, weight_out = weights
     channels, hidden = weight_in.shape
     block = NLON // 2
-    grad_rows = 2 * channels + hidden + 8
+    grad_rows = -(-(2 * channels + hidden + 3) // 64) * 64
     operands = [
-        state,
-        cot,
         table,
         back_table,
         split,
@@ -336,22 +331,29 @@
         weight_mid.T,
         weight_out.T,
     ]
+    if before is not None:
+        operands.append(before)
 
     def whole(shape):
         return pl.BlockSpec(shape, lambda i, j: (0,) * len(shape), pipeline_mode=pl.Buffered(1))
 
+    source = pl.BlockSpec(
+        (lat_count, groups, slots_here, rows, lanes),
+        lambda i, j: (0, 0, 0, sub, 0),
+        pipeline_mode=pl.Buffered(1),
+    )
     out_shapes = (
-        jax.ShapeDtypeStruct(state.shape, BF16),
+        jax.ShapeDtypeStruct((lat_count, groups, slots_here, rows, lanes), BF16),
         jax.ShapeDtypeStruct((grad_rows, hidden), F32),
     )
     wide = pltpu.VMEM((groups, slots * rows, lanes), F32)
     mat = pltpu.VMEM((2 * slots, channels), BF16)
     per_column = channels * hidden * 6 + hidden * hidden * 3 + 6 * slots * channels
     return pl.pallas_call(
-        functools.partial(column_kernel, rows, block),
+        functools.partial(column_kernel, rows, block, before is not None),
         out_shape=out_shapes,
         grid=(rows, NLON // block),
-        in_specs=[whole(o.shape) for o in operands],
+        in_specs=[source, source] + [whole(o.shape) for o in operands],
         out_specs=tuple(whole(o.shape) for o in out_shapes),
         scratch_shapes=[wide, wide, wide, mat, mat, pltpu.VMEM((2 * slots, channels), F32)],
         compiler_params=pltpu.CompilerParams(
@@ -359,14 +361,43 @@
         ),
         cost_estimate=pl.CostEstimate(
             flops=2 * rows * NLON * per_column,
-            bytes_accessed=6 * state.size + 4 * grad_rows * hidden,
+            bytes_accessed=6 * slots * rows * groups * lanes + 8 * grad_rows * hidden,
             transcendentals=2 * rows * NLON * hidden,
         ),
         name="columns",
-    )(*operands)
-
-
-def local(
+    )(state, cot, *operands)
+
+
+def swap(x, axis, bits):
+    return lax.ppermute(x, axis, [(i, i ^ bits) for i in range(lax.axis_size(axis))])
+
+
+def reduce_grads(total):
+    top = lax.axis_size("lat") // 4
+    steps = []
+    for axis, limit in (("lev", lax.axis_size("lev")), ("lat", top)):
+        bit = 1
+        while bit < limit:
+            steps.append((axis, bit))
+            bit *= 2
+    for axis, bit in steps:
+        size = total.shape[0] // 2
+        side = (lax.axis_index(axis) // bit) % 2
+        sent = lax.dynamic_slice_in_dim(total, (1 - side) * size, size).astype(BF16)
+        kept = lax.dynamic_slice_in_dim(total, side * size, size)
+        total = kept + swap(sent, axis, bit).astype(F32)
+    part = total.astype(BF16)
+    one, two, three = (swap(part, "lat", k * top).astype(F32) for k in (1, 2, 3))
+    part = ((part.astype(F32) + one) + (two + three)).astype(BF16)
+    for axis, bit in reversed(steps):
+        side = (lax.axis_index(axis) // bit) % 2
+        other = swap(part, axis, bit)
+        first, second = jnp.where(side == 0, part, other), jnp.where(side == 0, other, part)
+        part = jnp.concatenate([first, second], axis=0)
+    return part.astype(F32)
+
+
+def step(
     spec_in,
     cotangent,
     legendre_table,
@@ -401,6 +432,8 @@
 
     table = fourier_table(wave_order)
     split = split_parts(lanes)
+    rows = nlat // chunks // lat_count
+    subs = rows // 8
     received, before = [], None
     for k in range(chunks):
         state = legendre(own_waves, spec_rows, legendre_table, k, chunks, lat_count)
@@ -413,21 +446,22 @@
         cot = before = exchange(cot)
         received.append((state, cot))
     weights = (weight_in, bias_in, weight_mid, bias_mid, weight_out)
-    backs, totals = [], []
+    gain = norm_gain[None, :]
+    backs, total = [], None
     for state, cot in received:
-        back, grads = column_grads(
-            state, cot, table.T, table, split, split.T, norm_gain[None, :], weights
-        )
-        backs.append(exchange(back))
-        totals.append(grads)
-    summed = lax.psum(functools.reduce(jnp.add, totals), axes)
+        for sub in range(subs):
+            back, total = column_grads(
+                state, cot, sub, rows // subs, table.T, table, split, split.T, gain, weights, total
+            )
+            backs.append(exchange(back))
+    summed = reduce_grads(total)
     channels, hidden = weight_in.shape
     summed = summed * float(members * nlat * NLON) ** (-0.5)
     base = 2 * channels + hidden
     grad_w_in = summed[:channels]
     grad_w_mid = summed[channels : channels + hidden]
     grad_w_out = summed[channels + hidden : base].T
-    grad_spec = inverse_legendre(own_waves, cot_rows, legendre_table, factor, backs)
+    grad_spec = inverse_legendre(own_waves, cot_rows, legendre_table, factor, backs, subs)
     return (
         grad_spec.reshape(spec_in.shape),
         summed[base + 2, :channels],
@@ -446,7 +480,7 @@
         P("lat", None, None),
     ) + (P(),) * 8
     return jax.shard_map(
-        local,
+        step,
         mesh=mesh,
         in_specs=placed,
         out_specs=(P("lat", None, None, "lev"),) + (P(),) * 6,

time: 618 us -> 530 us (0.86)
  waiting for transfers between devices: 352 us -> 252 us
  starting transfers between devices: 31.4 us -> 53.9 us
  between operations: 14.2 us -> 0.89 us
    psum x1 -> x0, waiting for transfers between devices: 162 us -> none  [local(): summed = lax.psum(functools.reduce(jnp.add, totals), axes)]
    ppermute x0 -> x9, waiting for transfers between devices: none -> 36.2 us  [swap(): lax.ppermute(x, axis, [(i, i ^ bits) for i in range(lax.axis_size(axis))])]
    all_to_all x6 -> x8, waiting for transfers between devices: 190 us -> 216 us  [exchange(): x = lax.all_to_all(x, axes, split_axis=0, concat_axis=0, tiled=True)]
    ppermute x0 -> x9, starting transfers between devices: none -> 14.7 us  [swap(): lax.ppermute(x, axis, [(i, i ^ bits) for i in range(lax.axis_size(axis))])]
    all_to_all x6 -> x8, starting transfers between devices: 31.4 us -> 39.2 us  [exchange(): x = lax.all_to_all(x, axes, split_axis=0, concat_axis=0, tiled=True)]
    pallas_call x2 -> x4, Pallas kernels: 151 us -> 151 us  [column_grads(): pl.pallas_call(functools.partial(column_kernel, rows, block, before is no...]
  transfers between devices with their start and end apart: 7 -> 17, of which waited for: 4 -> 13; matrix products, arithmetic and copies ran while one was open for 3% -> 4% of each run, Pallas kernels for 28% -> 33%
where the time goes in v2:
time: 530 us; the launch traced here: 528 us
  waiting for transfers between devices  252 us (48%)
  Pallas kernels  191 us (36%)
  starting transfers between devices  53.9 us (10%)
  local copies, waits for them, and re-layouts  22 us (4%)
  other arithmetic  7.81 us (1%)
    all_to_all x8, waiting for transfers between devices, exchange(): x = lax.all_to_all(x, axes, split_axis=0, concat_axis=0, tiled=True)  216 us
    pallas_call x4, Pallas kernels, column_grads(): pl.pallas_call(functools.partial(column_kernel, rows, block, before is no...  151 us
    all_to_all x8, starting transfers between devices, exchange(): x = lax.all_to_all(x, axes, split_axis=0, concat_axis=0, tiled=True)  39.2 us
    ppermute x9, waiting for transfers between devices, swap(): lax.ppermute(x, axis, [(i, i ^ bits) for i in range(lax.axis_size(axis))])  36.2 us
    pallas_call x4, Pallas kernels, legendre(): pl.pallas_call(functools.partial(legendre_kernel, pair, members, degrees,...  29.7 us
    unnamed x21, local copies, waits for them, and re-layouts  15.3 us
    ppermute x9, starting transfers between devices, swap(): lax.ppermute(x, axis, [(i, i ^ bits) for i in range(lax.axis_size(axis))])  14.7 us
  transfers between devices with their start and end apart: 17, of which 13 were waited for; matrix products, arithmetic and copies ran while one was open for 4% of the time, Pallas kernels for 33%

profile of v2, /device:TPU:0, one launch (start us, length us, event | category | flops | bytes accessed | tf_op | source)
XLA Modules:
  0.0 528.2 jit_solution(13306750953667973675)
XLA Ops:
  0.6 3.4 copy.61.leg_ref
  4.0 0.6 dynamic_slice.21.waves
  4.6 7.2 %legendre_state.2 = bf16[8,4,24,16,128]{4,3,2,1,0:T(8,128)(2,1)} custom-call(s32[24]{0:T(128)} %dynamic_slice.21.waves, bf16[16416,128]{1,0:T(8,128)(2,1)} %bitcast.36, bf16[24,171,256]{2,1,0:T(8,128)(2,1)} %copy.61.leg_ref), custom_call_target="tpu_custom_call" | custom-call | flops 537919488 | bytes 8398848 | tf_op jit(solution)/shard_map/legendre_state/pallas_call | solution.py:99
  11.8 7.3 %all-to-all-start = ((bf16[32,24,16,128]{3,2,1,0:T(8,128)(2,1)}), bf16[32,24,16,128]{3,2,1,0:T(8,128)(2,1)S(1)}, u32[]{:S(2)}, u32[]{:S(2)}) async-start(bf16[32,24,16,128]{3,2,1,0:T(8,128)(2,1)} %bitcast.41), calls=%async_computation | async-start | bytes 6291456 | tf_op jit(solution)/shard_map/all_to_all | solution.py:430
  19.1 0.8 copy.49.rest_1_
  19.9 0.7 fusion.28.rest_0_.factor_ref
  20.6 7.7 %legendre_cot.2 = bf16[8,4,24,16,128]{4,3,2,1,0:T(8,128)(2,1)} custom-call(s32[24]{0:T(128)} %dynamic_slice.21.waves, bf16[16416,128]{1,0:T(8,128)(2,1)} %bitcast.33, bf16[24,171,256]{2,1,0:T(8,128)(2,1)} %copy.61.leg_ref, f32[171,1]{1,0:T(8,128)} %fusion.28.rest_0_.factor_ref, f32[256,1]{1,0:T(8,128)} %copy.49.rest_1_), custom_call_target="tpu_custom_call" | custom-call | flops 537919488 | bytes 8398848 | tf_op jit(solution)/shard_map/legendre_cot/pallas_call | solution.py:99
  28.2 62.2 %all-to-all-done = bf16[32,24,16,128]{3,2,1,0:T(8,128)(2,1)S(1)} async-done(((bf16[32,24,16,128]{3,2,1,0:T(8,128)(2,1)}), bf16[32,24,16,128]{3,2,1,0:T(8,128)(2,1)S(1)}, u32[]{:S(2)}, u32[]{:S(2)}) %all-to-all-start) | async-done | bytes 3145760 | tf_op jit(solution)/shard_map/all_to_all | solution.py:430
  90.5 1.7 copy-done.4
  92.1 4.1 all-to-all-start.1
  96.3 7.3 %legendre_state.3 = bf16[8,4,24,16,128]{4,3,2,1,0:T(8,128)(2,1)} custom-call(s32[24]{0:T(128)} %dynamic_slice.21.waves, bf16[16416,128]{1,0:T(8,128)(2,1)} %bitcast.37, bf16[24,171,256]{2,1,0:T(8,128)(2,1)} %copy.61.leg_ref), custom_call_target="tpu_custom_call" | custom-call | flops 537919488 | bytes 8398848 | tf_op jit(solution)/shard_map/legendre_state/pallas_call | solution.py:99
  103.5 64.1 %all-to-all-done.1 = bf16[32,24,16,128]{3,2,1,0:T(8,128)(2,1)} async-done(((bf16[32,24,16,128]{3,2,1,0:T(8,128)(2,1)}), bf16[32,24,16,128]{3,2,1,0:T(8,128)(2,1)}, u32[]{:S(2)}, u32[]{:S(2)}) %all-to-all-start.1) | async-done | bytes 3145760 | tf_op jit(solution)/shard_map/all_to_all | solution.py:430
  167.6 4.0 all-to-all-start.4
  171.6 1.9 multiply_convert_fusion.1
  173.6 0.8 pad_maximum_fusion.1
  174.4 0.9 copy.55.table_ref
  175.3 1.8 copy.52
  177.1 2.0 copy.53
  179.1 1.8 copy.54
  180.9 1.0 fusion.22
  181.9 37.1 %columns.4 = (bf16[8,4,24,8,128]{4,3,2,1,0:T(8,128)(2,1)}, f32[1088,512]{1,0:T(8,128)}) custom-call(bf16[8,4,24,16,128]{4,3,2,1,0:T(8,128)(2,1)} %bitcast.48, bf16[8,4,24,16,128]{4,3,2,1,0:T(8,128)(2,1)} %bitcast.6.cot_ref, bf16[512,384]{1,0:T(8,128)(2,1)} %copy.55.table_ref, bf16[384,512]{1,0:T(8,128)(2,1)} %get-tuple-element.64.back_table_ref, ...), custom_call_target="tpu_custom_call" | custom-call | flops 15300820992 | bytes 9175040 | tf_op jit(solution)/shard_map/columns/pallas_call | solution.py:352
  219.0 23.9 %all-to-all-done.4 = bf16[32,24,16,128]{3,2,1,0:T(8,128)(2,1)S(1)} async-done(((bf16[32,24,16,128]{3,2,1,0:T(8,128)(2,1)}), bf16[32,24,16,128]{3,2,1,0:T(8,128)(2,1)S(1)}, u32[]{:S(2)}, u32[]{:S(2)}) %all-to-all-start.4) | async-done | bytes 3145760 | tf_op jit(solution)/shard_map/all_to_all | solution.py:430
  243.0 1.6 copy-done.3
  244.6 4.0 all-to-all-start.2
  248.6 7.6 %legendre_cot.3 = bf16[8,4,24,16,128]{4,3,2,1,0:T(8,128)(2,1)} custom-call(s32[24]{0:T(128)} %dynamic_slice.21.waves, bf16[16416,128]{1,0:T(8,128)(2,1)} %bitcast.34, bf16[24,171,256]{2,1,0:T(8,128)(2,1)} %copy.61.leg_ref, f32[171,1]{1,0:T(8,128)} %fusion.28.rest_0_.factor_ref, f32[256,1]{1,0:T(8,128)} %copy.49.rest_1_), custom_call_target="tpu_custom_call" | custom-call | flops 537919488 | bytes 8398848 | tf_op jit(solution)/shard_map/legendre_cot/pallas_call | solution.py:99
  256.3 30.0 %all-to-all-done.2 = bf16[32,24,8,128]{3,2,1,0:T(8,128)(2,1)S(1)} async-done(((bf16[32,24,8,128]{3,2,1,0:T(8,128)(2,1)}), bf16[32,24,8,128]{3,2,1,0:T(8,128)(2,1)S(1)}, u32[]{:S(2)}, u32[]{:S(2)}) %all-to-all-start.2) | async-done | bytes 1572896 | tf_op jit(solution)/shard_map/all_to_all | solution.py:430
  286.3 1.1 copy-done
  287.4 3.9 all-to-all-start.5
  291.4 38.1 %columns.5 = (bf16[8,4,24,8,128]{4,3,2,1,0:T(8,128)(2,1)}, f32[1088,512]{1,0:T(8,128)}) custom-call(bf16[8,4,24,16,128]{4,3,2,1,0:T(8,128)(2,1)} %bitcast.49, bf16[8,4,24,16,128]{4,3,2,1,0:T(8,128)(2,1)} %bitcast.6.cot_ref, bf16[512,384]{1,0:T(8,128)(2,1)} %copy.55.table_ref, bf16[384,512]{1,0:T(8,128)(2,1)} %get-tuple-element.64.back_table_ref, ...), custom_call_target="tpu_custom_call" | custom-call | flops 15300820992 | bytes 9175040 | tf_op jit(solution)/shard_map/columns/pallas_call | solution.py:352
  329.4 33.3 %all-to-all-done.5 = bf16[32,24,16,128]{3,2,1,0:T(8,128)(2,1)} async-done(((bf16[32,24,16,128]{3,2,1,0:T(8,128)(2,1)}), bf16[32,24,16,128]{3,2,1,0:T(8,128)(2,1)}, u32[]{:S(2)}, u32[]{:S(2)}) %all-to-all-start.5) | async-done | bytes 3145760 | tf_op jit(solution)/shard_map/all_to_all | solution.py:430
  362.7 4.0 all-to-all-start.3
  366.7 38.0 %columns.6 = (bf16[8,4,24,8,128]{4,3,2,1,0:T(8,128)(2,1)}, f32[1088,512]{1,0:T(8,128)}) custom-call(bf16[8,4,24,16,128]{4,3,2,1,0:T(8,128)(2,1)} %bitcast.46, bf16[8,4,24,16,128]{4,3,2,1,0:T(8,128)(2,1)} %bitcast.21.cot_ref, bf16[512,384]{1,0:T(8,128)(2,1)} %copy.55.table_ref, bf16[384,512]{1,0:T(8,128)(2,1)} %get-tuple-element.64.back_table_ref, ...), custom_call_target="tpu_custom_call" | custom-call | flops 15300820992 | bytes 9175040 | tf_op jit(solution)/shard_map/columns/pallas_call | solution.py:352
  404.8 5.8 %all-to-all-start.6 = ((bf16[32,24,8,128]{3,2,1,0:T(8,128)(2,1)}), bf16[32,24,8,128]{3,2,1,0:T(8,128)(2,1)S(1)}, u32[]{:S(2)}, u32[]{:S(2)}) async-start(bf16[32,24,8,128]{3,2,1,0:T(8,128)(2,1)} %bitcast.51), calls=%async_computation.6 | async-start | bytes 3145728 | tf_op jit(solution)/shard_map/all_to_all | solution.py:430
  410.6 38.1 %columns.7 = (bf16[8,4,24,8,128]{4,3,2,1,0:T(8,128)(2,1)}, f32[1088,512]{1,0:T(8,128)}) custom-call(bf16[8,4,24,16,128]{4,3,2,1,0:T(8,128)(2,1)} %bitcast.47, bf16[8,4,24,16,128]{4,3,2,1,0:T(8,128)(2,1)} %bitcast.21.cot_ref, bf16[512,384]{1,0:T(8,128)(2,1)} %copy.55.table_ref, bf16[384,512]{1,0:T(8,128)(2,1)} %get-tuple-element.64.back_table_ref, ...), custom_call_target="tpu_custom_call" | custom-call | flops 15300820992 | bytes 9175040 | tf_op jit(solution)/shard_map/columns/pallas_call | solution.py:352
  448.7 1.3 dynamic-slice_convert_fusion
  450.0 0.3 collective-permute-start
  450.3 1.9 collective-permute-done
  452.2 1.6 convert_add_fusion
  453.8 1.8 collective-permute-start.1
  455.7 7.0 %collective-permute-done.1 = bf16[272,512]{1,0:T(8,128)(2,1)S(1)} collective-permute-done((bf16[272,512]{1,0:T(8,128)(2,1)S(1)}, bf16[272,512]{1,0:T(8,128)(2,1)S(1)}, u32[]{:S(2)}, u32[]{:S(2)}) %collective-permute-start.1) | collective-permute-done | bytes 278560 | tf_op jit(solution)/shard_map/ppermute | solution.py:372
  462.8 0.8 copy-done.5
  463.6 1.7 collective-permute-start.2
  465.3 3.4 collective-permute-done.2
  468.7 1.0 add_convert_fusion.1
  469.7 3.6 collective-permute-start.5
  473.3 0.9 collective-permute-start.3
  474.2 5.9 %all-to-all-start.7 = ((bf16[32,24,8,128]{3,2,1,0:T(8,128)(2,1)}), bf16[32,24,8,128]{3,2,1,0:T(8,128)(2,1)}, u32[]{:S(2)}, u32[]{:S(2)}) async-start(bf16[32,24,8,128]{3,2,1,0:T(8,128)(2,1)} %bitcast.50), calls=%async_computation.7 | async-start | bytes 3145728 | tf_op jit(solution)/shard_map/all_to_all | solution.py:430
  480.1 3.6 collective-permute-done.4
  483.7 1.5 collective-permute-start.6
  485.3 8.4 %collective-permute-done.6 = bf16[136,512]{1,0:T(8,128)(2,1)S(1)} collective-permute-done((bf16[136,512]{1,0:T(8,128)(2,1)S(1)}, bf16[136,512]{1,0:T(8,128)(2,1)S(1)}, u32[]{:S(2)}, u32[]{:S(2)}) %collective-permute-start.6) | collective-permute-done | bytes 139296 | tf_op jit(solution)/shard_map/ppermute | solution.py:372
  493.7 4.6 collective-permute-start.7
  498.3 10.2 %collective-permute-done.7 = bf16[272,512]{1,0:T(8,128)(2,1)S(1)} collective-permute-done((bf16[272,512]{1,0:T(8,128)(2,1)S(1)}, bf16[272,512]{1,0:T(8,128)(2,1)S(1)}, u32[]{:S(2)}, u32[]{:S(2)}) %collective-permute-start.7) | collective-permute-done | bytes 278560 | tf_op jit(solution)/shard_map/ppermute | solution.py:372
  508.5 0.1 broadcast_select_fusion.3
  508.7 0.2 collective-permute-start.8
  508.9 1.8 collective-permute-done.8
  510.7 0.2 broadcast_select_fusion.1
  510.9 0.3 convert_multiply_fusion
  511.2 0.6 slice.24
  511.8 1.0 slice.27
  512.8 0.9 slice_bitcast_fusion
  513.7 1.0 copy.62
  514.7 0.6 fusion.32
  515.2 2.6 all-to-all-done.7
  517.9 10.4 %inverse_legendre.1 = f32[16416,128]{1,0:T(8,128)} custom-call(s32[24]{0:T(128)} %dynamic_slice.21.waves, bf16[16416,128]{1,0:T(8,128)(2,1)} %bitcast.35, bf16[24,171,256]{2,1,0:T(8,128)(2,1)} %copy.61.leg_ref, f32[171,1]{1,0:T(8,128)} %fusion.28.rest_0_.factor_ref, bf16[8,4,24,8,128]{4,3,2,1,0:T(8,128)(2,1)} %bitcast.43, ...), custom_call_target="tpu_custom_call" | custom-call | flops 1075838976 | bytes 21000192 | tf_op jit(solution)/shard_map/inverse_legendre/pallas_call | solution.py:156
  (28 shorter events, 0.4 us)
Async XLA Ops:
  0.6 3.4 copy-start.6
  11.8 7.3 %copy-start.7 = (f32[256]{0:T(256)S(1)}, f32[256]{0:T(256)}, u32[]{:S(2)}) copy-start(f32[256]{0:T(256)} %param.14) | copy-start | bytes 3076
  11.8 78.7 %all-to-all-start = ((bf16[32,24,16,128]{3,2,1,0:T(8,128)(2,1)}), bf16[32,24,16,128]{3,2,1,0:T(8,128)(2,1)S(1)}, u32[]{:S(2)}, u32[]{:S(2)}) async-start(bf16[32,24,16,128]{3,2,1,0:T(8,128)(2,1)} %bitcast.41), calls=%async_computation | async-start | bytes 6291456 | tf_op jit(solution)/shard_map/all_to_all | solution.py:430
  90.5 1.7 copy-start.4
  92.1 75.5 %all-to-all-start.1 = ((bf16[32,24,16,128]{3,2,1,0:T(8,128)(2,1)}), bf16[32,24,16,128]{3,2,1,0:T(8,128)(2,1)}, u32[]{:S(2)}, u32[]{:S(2)}) async-start(bf16[32,24,16,128]{3,2,1,0:T(8,128)(2,1)} %bitcast.39), calls=%async_computation.1 | async-start | bytes 6291456 | tf_op jit(solution)/shard_map/all_to_all | solution.py:430
  167.6 75.4 %all-to-all-start.4 = ((bf16[32,24,16,128]{3,2,1,0:T(8,128)(2,1)}), bf16[32,24,16,128]{3,2,1,0:T(8,128)(2,1)S(1)}, u32[]{:S(2)}, u32[]{:S(2)}) async-start(bf16[32,24,16,128]{3,2,1,0:T(8,128)(2,1)} %bitcast.40), calls=%async_computation.4 | async-start | bytes 6291456 | tf_op jit(solution)/shard_map/all_to_all | solution.py:430
  243.0 1.6 copy-start.3
  244.6 41.7 %all-to-all-start.2 = ((bf16[32,24,8,128]{3,2,1,0:T(8,128)(2,1)}), bf16[32,24,8,128]{3,2,1,0:T(8,128)(2,1)S(1)}, u32[]{:S(2)}, u32[]{:S(2)}) async-start(bf16[32,24,8,128]{3,2,1,0:T(8,128)(2,1)} %bitcast.53), calls=%async_computation.2 | async-start | bytes 3145728 | tf_op jit(solution)/shard_map/all_to_all | solution.py:430
  286.3 1.2 copy-start
  287.4 75.2 %all-to-all-start.5 = ((bf16[32,24,16,128]{3,2,1,0:T(8,128)(2,1)}), bf16[32,24,16,128]{3,2,1,0:T(8,128)(2,1)}, u32[]{:S(2)}, u32[]{:S(2)}) async-start(bf16[32,24,16,128]{3,2,1,0:T(8,128)(2,1)} %bitcast.38), calls=%async_computation.5 | async-start | bytes 6291456 | tf_op jit(solution)/shard_map/all_to_all | solution.py:430
  362.7 42.1 %all-to-all-start.3 = ((bf16[32,24,8,128]{3,2,1,0:T(8,128)(2,1)}), bf16[32,24,8,128]{3,2,1,0:T(8,128)(2,1)S(1)}, u32[]{:S(2)}, u32[]{:S(2)}) async-start(bf16[32,24,8,128]{3,2,1,0:T(8,128)(2,1)} %bitcast.52), calls=%async_computation.3 | async-start | bytes 3145728 | tf_op jit(solution)/shard_map/all_to_all | solution.py:430
  404.8 43.9 %copy-start.1 = (bf16[32,24,8,128]{3,2,1,0:T(8,128)(2,1)}, bf16[32,24,8,128]{3,2,1,0:T(8,128)(2,1)S(1)}, u32[]{:S(2)}) copy-start(bf16[32,24,8,128]{3,2,1,0:T(8,128)(2,1)S(1)} %all-to-all-done.3) | copy-start | bytes 4718596
  404.8 69.4 %all-to-all-start.6 = ((bf16[32,24,8,128]{3,2,1,0:T(8,128)(2,1)}), bf16[32,24,8,128]{3,2,1,0:T(8,128)(2,1)S(1)}, u32[]{:S(2)}, u32[]{:S(2)}) async-start(bf16[32,24,8,128]{3,2,1,0:T(8,128)(2,1)} %bitcast.51), calls=%async_computation.6 | async-start | bytes 3145728 | tf_op jit(solution)/shard_map/all_to_all | solution.py:430
  450.0 2.2 collective-permute-start
  453.8 8.9 %collective-permute-start.1 = (bf16[272,512]{1,0:T(8,128)(2,1)S(1)}, bf16[272,512]{1,0:T(8,128)(2,1)S(1)}, u32[]{:S(2)}, u32[]{:S(2)}) collective-permute-start(bf16[272,512]{1,0:T(8,128)(2,1)S(1)} %dynamic-slice_convert_fusion.1), channel_id=1, source_target_pairs={{0,2},{1,3},{2,0},{3,1},{4,6},{5,7},{6,4},{7,5},{8,10},{9,11},{10,... | collective-permute-start | bytes 835592 | tf_op jit(solution)/shard_map/ppermute | solution.py:372
  462.8 0.8 copy-start.5
  463.6 5.1 collective-permute-start.2
  469.7 10.3 %collective-permute-start.5 = (bf16[136,512]{1,0:T(8,128)(2,1)S(1)}, bf16[136,512]{1,0:T(8,128)(2,1)S(1)}, u32[]{:S(2)}, u32[]{:S(2)}) collective-permute-start(bf16[136,512]{1,0:T(8,128)(2,1)S(1)} %add_convert_fusion.1), channel_id=1, source_target_pairs={{0,24},{4,28},{8,16},{12,20},{16,8},{20,12},{24,0},{28,4},{1,25},{... | collective-permute-start | bytes 417800 | tf_op jit(solution)/shard_map/ppermute | solution.py:372
  473.3 10.3 %collective-permute-start.4 = (bf16[136,512]{1,0:T(8,128)(2,1)S(1)}, bf16[136,512]{1,0:T(8,128)(2,1)S(1)}, u32[]{:S(2)}, u32[]{:S(2)}) collective-permute-start(bf16[136,512]{1,0:T(8,128)(2,1)S(1)} %add_convert_fusion.1), channel_id=1, source_target_pairs={{0,16},{4,20},{8,24},{12,28},{16,0},{20,4},{24,8},{28,12},{1,17},{... | collective-permute-start | bytes 417800 | tf_op jit(solution)/shard_map/ppermute | solution.py:372
  473.3 10.3 %collective-permute-start.3 = (bf16[136,512]{1,0:T(8,128)(2,1)S(1)}, bf16[136,512]{1,0:T(8,128)(2,1)S(1)}, u32[]{:S(2)}, u32[]{:S(2)}) collective-permute-start(bf16[136,512]{1,0:T(8,128)(2,1)S(1)} %add_convert_fusion.1), channel_id=1, source_target_pairs={{0,8},{4,12},{8,0},{12,4},{16,24},{20,28},{24,16},{28,20},{1,9},{5... | collective-permute-start | bytes 417800 | tf_op jit(solution)/shard_map/ppermute | solution.py:372
  474.2 19.5 %copy-start.2 = (bf16[32,24,8,128]{3,2,1,0:T(8,128)(2,1)}, bf16[32,24,8,128]{3,2,1,0:T(8,128)(2,1)S(1)}, u32[]{:S(2)}) copy-start(bf16[32,24,8,128]{3,2,1,0:T(8,128)(2,1)S(1)} %all-to-all-done.6) | copy-start | bytes 4718596
  474.2 43.7 %all-to-all-start.7 = ((bf16[32,24,8,128]{3,2,1,0:T(8,128)(2,1)}), bf16[32,24,8,128]{3,2,1,0:T(8,128)(2,1)}, u32[]{:S(2)}, u32[]{:S(2)}) async-start(bf16[32,24,8,128]{3,2,1,0:T(8,128)(2,1)} %bitcast.50), calls=%async_computation.7 | async-start | bytes 3145728 | tf_op jit(solution)/shard_map/all_to_all | solution.py:430
  483.7 9.9 %collective-permute-start.6 = (bf16[136,512]{1,0:T(8,128)(2,1)S(1)}, bf16[136,512]{1,0:T(8,128)(2,1)S(1)}, u32[]{:S(2)}, u32[]{:S(2)}) collective-permute-start(bf16[136,512]{1,0:T(8,128)(2,1)S(1)} %add_convert_fusion), channel_id=1, source_target_pairs={{0,4},{4,0},{8,12},{12,8},{16,20},{20,16},{24,28},{28,24},{1,5},{5... | collective-permute-start | bytes 417800 | tf_op jit(solution)/shard_map/ppermute | solution.py:372
  493.7 14.8 %collective-permute-start.7 = (bf16[272,512]{1,0:T(8,128)(2,1)S(1)}, bf16[272,512]{1,0:T(8,128)(2,1)S(1)}, u32[]{:S(2)}, u32[]{:S(2)}) collective-permute-start(bf16[272,512]{1,0:T(8,128)(2,1)S(1)} %pad_maximum_fusion.2), channel_id=1, source_target_pairs={{0,2},{1,3},{2,0},{3,1},{4,6},{5,7},{6,4},{7,5},{8,10},{9,11},{10,... | collective-permute-start | bytes 835592 | tf_op jit(solution)/shard_map/ppermute | solution.py:372
  508.7 2.0 collective-permute-start.8

commit v3 on v2

--- a/solution.py
+++ b/solution.py
@@ -49,82 +49,79 @@
     return lax.dot_general(left, right, (((0,), (0,)), ((), ())), preferred_element_type=F32)
 
 
-def legendre_kernel(pair, members, degrees, is_cot, waves, x_ref, leg_ref, *rest):
-    if is_cot:
-        factor_ref, quad_ref, out_ref, wide = rest
-    else:
-        out_ref, wide = rest
+def legendre_kernel(
+    pair, members, degrees, waves, x_ref, y_ref, leg_ref, factor_ref, quad_ref, out_ref, x_wide, y_wide
+):
     step = pl.program_id(0)
-    wide[...] = x_ref[...].astype(F32)
-    lat_count, _, _, rows, lanes = out_ref.shape
+    x_wide[...] = x_ref[...].astype(F32)
+    y_wide[...] = y_ref[...].astype(F32)
+    lat_count, _, _, _, rows, lanes = out_ref.shape
     for k in range(pair):
         m = waves[step * pair + k]
         degree = lax.broadcasted_iota(jnp.int32, leg_ref.shape[1:], 0)
         living = (degree >= m) & (m < WAVES)
         basis = jnp.where(living, leg_ref[k].astype(F32), 0.0).astype(BF16)
-        parts = []
-        for e in range(members):
-            part = wide[pl.ds(k * degrees * members + e, degrees, stride=members), :]
+        for is_cot, wide in enumerate((x_wide, y_wide)):
+            parts = []
+            for e in range(members):
+                part = wide[pl.ds(k * degrees * members + e, degrees, stride=members), :]
+                if is_cot:
+                    part = TIME_STEP * part * factor_ref[...]
+                parts.append(part.astype(BF16))
+            result = dot_rows(basis, jnp.concatenate(parts, axis=1))
             if is_cot:
-                part = TIME_STEP * part * factor_ref[...]
-            parts.append(part.astype(BF16))
-        result = dot_rows(basis, jnp.concatenate(parts, axis=1))
-        if is_cot:
-            result = result * quad_ref[...]
-        result = result.astype(BF16)
-        for e in range(members):
-            out_ref[:, e, k] = result[:, e * lanes : (e + 1) * lanes].reshape(lat_count, rows, lanes)
-
-
-def legendre(waves, packed, legendre_table, chunk, chunks, lat_count, factor=None, quad=None):
+                result = result * quad_ref[...]
+            result = result.astype(BF16)
+            for e in range(members):
+                out_ref[:, e, is_cot, k] = result[:, e * lanes : (e + 1) * lanes].reshape(
+                    lat_count, rows, lanes
+                )
+
+
+def legendre(waves, spec, cot, legendre_table, chunk, chunks, lat_count, factor, quad):
     slots, degrees, nlat = legendre_table.shape
-    lanes = packed.shape[1]
-    members = packed.shape[0] // (slots * degrees)
+    lanes = spec.shape[1]
+    members = spec.shape[0] // (slots * degrees)
     pair = 4 if slots % 4 == 0 else 2
     span = nlat // chunks
     rows = span // lat_count
-    is_cot = factor is not None
     block = pair * degrees * members
-    in_specs = [
-        pl.BlockSpec((block, lanes), lambda i, w: (i, 0)),
-        pl.BlockSpec((pair, degrees, span), lambda i, w: (i, 0, chunk)),
-    ]
-    operands = [packed, legendre_table]
-    if is_cot:
-        in_specs += [
-            pl.BlockSpec((degrees, 1), lambda i, w: (0, 0)),
-            pl.BlockSpec((span, 1), lambda i, w: (chunk, 0)),
-        ]
-        operands += [factor, quad]
+    packed = pl.BlockSpec((block, lanes), lambda i, w: (i, 0))
     return pl.pallas_call(
-        functools.partial(legendre_kernel, pair, members, degrees, is_cot),
-        out_shape=jax.ShapeDtypeStruct((lat_count, members, slots, rows, lanes), BF16),
+        functools.partial(legendre_kernel, pair, members, degrees),
+        out_shape=jax.ShapeDtypeStruct((lat_count, members, 2, slots, rows, lanes), BF16),
         grid_spec=pltpu.PrefetchScalarGridSpec(
             num_scalar_prefetch=1,
             grid=(slots // pair,),
-            in_specs=in_specs,
+            in_specs=[
+                packed,
+                packed,
+                pl.BlockSpec((pair, degrees, span), lambda i, w: (i, 0, chunk)),
+                pl.BlockSpec((degrees, 1), lambda i, w: (0, 0)),
+                pl.BlockSpec((span, 1), lambda i, w: (chunk, 0)),
+            ],
             out_specs=pl.BlockSpec(
-                (lat_count, members, pair, rows, lanes), lambda i, w: (0, 0, i, 0, 0)
+                (lat_count, members, 2, pair, rows, lanes), lambda i, w: (0, 0, 0, i, 0, 0)
             ),
-            scratch_shapes=[pltpu.VMEM((block, lanes), F32)],
+            scratch_shapes=[pltpu.VMEM((block, lanes), F32)] * 2,
         ),
         compiler_params=pltpu.CompilerParams(
             dimension_semantics=("arbitrary",), vmem_limit_bytes=60 << 20
         ),
         cost_estimate=pl.CostEstimate(
-            flops=2 * slots * degrees * span * members * lanes,
-            bytes_accessed=2 * packed.size + 2 * slots * span * (degrees + members * lanes),
+            flops=4 * slots * degrees * span * members * lanes,
+            bytes_accessed=4 * spec.size + 2 * slots * span * (degrees + 2 * members * lanes),
             transcendentals=0,
         ),
-        name="legendre_cot" if is_cot else "legendre_state",
-    )(waves, *operands)
-
-
-def inverse_kernel(pair, members, degrees, subs, waves, cot_ref, leg_ref, factor_ref, *rest):
+        name="legendre",
+    )(waves, spec, cot, legendre_table, factor, quad)
+
+
+def inverse_kernel(pair, members, degrees, counts, waves, cot_ref, leg_ref, factor_ref, *rest):
     *backs, out_ref, wide = rest
     step = pl.program_id(0)
     wide[...] = cot_ref[...].astype(F32)
-    lat_count, _, _, rows, lanes = backs[0].shape
+    lanes = cot_ref.shape[1]
     for k in range(pair):
         m = waves[step * pair + k]
         degree = lax.broadcasted_iota(jnp.int32, leg_ref.shape[1:], 0)
@@ -133,11 +130,11 @@
         shrink = jnp.where((column >= m) & (m < WAVES), factor_ref[...], 0.0)
         sides = []
         for e in range(members):
-            pieces = []
-            for first in range(0, len(backs), subs):
-                subrows = [b[:, e, k].astype(F32) for b in backs[first : first + subs]]
-                joined = jnp.concatenate(subrows, axis=1)
-                pieces.append(joined.reshape(lat_count * subs * rows, lanes))
+            pieces, rest_backs = [], list(backs)
+            for subs in counts:
+                joined = [rest_backs.pop(0)[:, e, k].astype(F32) for _ in range(subs)]
+                joined = jnp.concatenate(joined, axis=1) if subs > 1 else joined[0]
+                pieces.append(joined.reshape(-1, lanes))
             sides.append(jnp.concatenate(pieces, axis=0).astype(BF16))
         result = dot(basis, jnp.concatenate(sides, axis=1))
         for e in range(members):
@@ -145,16 +142,14 @@
             out_ref[where, :] = wide[where, :] * shrink + result[:, e * lanes : (e + 1) * lanes]
 
 
-def inverse_legendre(waves, packed, legendre_table, factor, backs, subs):
+def inverse_legendre(waves, packed, legendre_table, factor, backs, counts):
     slots, degrees, nlat = legendre_table.shape
     lanes = packed.shape[1]
     members = packed.shape[0] // (slots * degrees)
     pair = 4 if slots % 4 == 0 else 2
     block = pair * degrees * members
-    lat_count, _, _, rows, _ = backs[0].shape
-    chunks = len(backs)
     return pl.pallas_call(
-        functools.partial(inverse_kernel, pair, members, degrees, subs),
+        functools.partial(inverse_kernel, pair, members, degrees, counts),
         out_shape=jax.ShapeDtypeStruct(packed.shape, F32),
         grid_spec=pltpu.PrefetchScalarGridSpec(
             num_scalar_prefetch=1,
@@ -165,9 +160,9 @@
                 pl.BlockSpec((degrees, 1), lambda i, w: (0, 0)),
             ]
             + [
-                pl.BlockSpec((lat_count, members, pair, rows, lanes), lambda i, w: (0, 0, i, 0, 0))
-            ]
-            * chunks,
+                pl.BlockSpec(b.shape[:2] + (pair,) + b.shape[3:], lambda i, w: (0, 0, i, 0, 0))
+                for b in backs
+            ],
             out_specs=pl.BlockSpec((block, lanes), lambda i, w: (i, 0)),
             scratch_shapes=[pltpu.VMEM((block, lanes), F32)],
         ),
@@ -310,8 +305,8 @@
                 out_ref[i, j] = out_wide[j, where, :].astype(BF16).reshape(slots_here, rows, lanes)
 
 
-def column_grads(state, cot, sub, rows, table, back_table, split, merge, gain, weights, before):
-    lat_count, groups, slots_here, _, lanes = state.shape
+def column_grads(pair, sub, rows, table, back_table, split, merge, gain, weights, before):
+    lat_count, groups, _, slots_here, _, lanes = pair.shape
     slots = lat_count * slots_here
     weight_in, bias_in, weight_mid, bias_mid, weight_out = weights
     channels, hidden = weight_in.shape
@@ -337,11 +332,13 @@
     def whole(shape):
         return pl.BlockSpec(shape, lambda i, j: (0,) * len(shape), pipeline_mode=pl.Buffered(1))
 
-    source = pl.BlockSpec(
-        (lat_count, groups, slots_here, rows, lanes),
-        lambda i, j: (0, 0, 0, sub, 0),
-        pipeline_mode=pl.Buffered(1),
-    )
+    def source(which):
+        return pl.BlockSpec(
+            (lat_count, groups, None, slots_here, rows, lanes),
+            lambda i, j: (0, 0, which, 0, sub, 0),
+            pipeline_mode=pl.Buffered(1),
+        )
+
     out_shapes = (
         jax.ShapeDtypeStruct((lat_count, groups, slots_here, rows, lanes), BF16),
         jax.ShapeDtypeStruct((grad_rows, hidden), F32),
@@ -353,7 +350,7 @@
         functools.partial(column_kernel, rows, block, before is not None),
         out_shape=out_shapes,
         grid=(rows, NLON // block),
-        in_specs=[source, source] + [whole(o.shape) for o in operands],
+        in_specs=[source(0), source(1)] + [whole(o.shape) for o in operands],
         out_specs=tuple(whole(o.shape) for o in out_shapes),
         scratch_shapes=[wide, wide, wide, mat, mat, pltpu.VMEM((2 * slots, channels), F32)],
         compiler_params=pltpu.CompilerParams(
@@ -365,7 +362,7 @@
             transcendentals=2 * rows * NLON * hidden,
         ),
         name="columns",
-    )(state, cot, *operands)
+    )(pair, pair, *operands)
 
 
 def swap(x, axis, bits):
@@ -434,24 +431,22 @@
     split = split_parts(lanes)
     rows = nlat // chunks // lat_count
     subs = rows // 8
-    received, before = [], None
+    received = []
     for k in range(chunks):
-        state = legendre(own_waves, spec_rows, legendre_table, k, chunks, lat_count)
-        if before is not None:
-            state, before = lax.optimization_barrier((state, before))
-            received[-1] = (received[-1][0], before)
-        state = exchange(state)
-        cot = legendre(own_waves, cot_rows, legendre_table, k, chunks, lat_count, factor, quad)
-        cot, state = lax.optimization_barrier((cot, state))
-        cot = before = exchange(cot)
-        received.append((state, cot))
+        pair = legendre(
+            own_waves, spec_rows, cot_rows, legendre_table, k, chunks, lat_count, factor, quad
+        )
+        if received:
+            pair, received[-1] = lax.optimization_barrier((pair, received[-1]))
+        received.append(exchange(pair))
     weights = (weight_in, bias_in, weight_mid, bias_mid, weight_out)
     gain = norm_gain[None, :]
+    counts = (1,) * (chunks - 1) + (subs,)
     backs, total = [], None
-    for state, cot in received:
-        for sub in range(subs):
+    for k, pair in enumerate(received):
+        for sub in range(counts[k]):
             back, total = column_grads(
-                state, cot, sub, rows // subs, table.T, table, split, split.T, gain, weights, total
+                pair, sub, rows // counts[k], table.T, table, split, split.T, gain, weights, total
             )
             backs.append(exchange(back))
     summed = reduce_grads(total)
@@ -461,7 +456,7 @@
     grad_w_in = summed[:channels]
     grad_w_mid = summed[channels : channels + hidden]
     grad_w_out = summed[channels + hidden : base].T
-    grad_spec = inverse_legendre(own_waves, cot_rows, legendre_table, factor, backs, subs)
+    grad_spec = inverse_legendre(own_waves, cot_rows, legendre_table, factor, backs, counts)
     return (
         grad_spec.reshape(spec_in.shape),
         summed[base + 2, :channels],

time: 530 us -> 489 us (0.923)
  starting transfers between devices: 53.9 us -> 35.9 us
  Pallas kernels: 191 us -> 183 us
  waiting for transfers between devices: 252 us -> 245 us
  local copies, waits for them, and re-layouts: 22 us -> 15.7 us
    all_to_all x8 -> x5, waiting for transfers between devices: 216 us -> 199 us  [exchange(): x = lax.all_to_all(x, axes, split_axis=0, concat_axis=0, tiled=True)]
    all_to_all x8 -> x5, starting transfers between devices: 39.2 us -> 23.5 us  [exchange(): x = lax.all_to_all(x, axes, split_axis=0, concat_axis=0, tiled=True)]
    ppermute x9, waiting for transfers between devices: 36.2 us -> 46.2 us  [swap(): lax.ppermute(x, axis, [(i, i ^ bits) for i in range(lax.axis_size(axis))])]
    pallas_call x4 -> x2, Pallas kernels: 29.7 us -> 20.2 us  [legendre(): pl.pallas_call(functools.partial(legendre_kernel, pair, members, degrees)...]
    unnamed x21 -> x19, local copies, waits for them, and re-layouts: 15.3 us -> 8.07 us
    pallas_call x4 -> x3, Pallas kernels: 151 us -> 152 us  [column_grads(): pl.pallas_call(functools.partial(column_kernel, rows, block, before is no...]
  transfers between devices with their start and end apart: 17 -> 14, of which waited for: 13 -> 10; matrix products, arithmetic and copies ran while one was open for 4% -> 4% of each run, Pallas kernels for 33% -> 33%
where the time goes in v3:
time: 489 us; the launch traced here: 488 us
  waiting for transfers between devices  245 us (50%)
  Pallas kernels  183 us (37%)
  starting transfers between devices  35.9 us (7%)
  local copies, waits for them, and re-layouts  15.7 us (3%)
  other arithmetic  7.89 us (2%)
    all_to_all x5, waiting for transfers between devices, exchange(): x = lax.all_to_all(x, axes, split_axis=0, concat_axis=0, tiled=True)  199 us
    pallas_call x3, Pallas kernels, column_grads(): pl.pallas_call(functools.partial(column_kernel, rows, block, before is no...  152 us
    ppermute x9, waiting for transfers between devices, swap(): lax.ppermute(x, axis, [(i, i ^ bits) for i in range(lax.axis_size(axis))])  46.2 us
    all_to_all x5, starting transfers between devices, exchange(): x = lax.all_to_all(x, axes, split_axis=0, concat_axis=0, tiled=True)  23.5 us
    pallas_call x2, Pallas kernels, legendre(): pl.pallas_call(functools.partial(legendre_kernel, pair, members, degrees)...  20.2 us
    ppermute x9, starting transfers between devices, swap(): lax.ppermute(x, axis, [(i, i ^ bits) for i in range(lax.axis_size(axis))])  12.4 us
    pallas_call x1, Pallas kernels, inverse_legendre(): pl.pallas_call(functools.partial(inverse_kernel, pair, members, degrees,...  10.4 us
  transfers between devices with their start and end apart: 14, of which 10 were waited for; matrix products, arithmetic and copies ran while one was open for 4% of the time, Pallas kernels for 33%

profile of v3, /device:TPU:0, one launch (start us, length us, event | category | flops | bytes accessed | tf_op | source)
XLA Modules:
  0.0 487.9 jit_solution(10906568891550400597)
XLA Ops:
  0.6 0.0 copy-start.6
  0.6 0.7 fusion.28.factor_ref
  1.3 3.4 copy.52.leg_ref
  4.7 0.8 copy.43.quad_ref
  5.5 0.6 dynamic_slice.21.waves
  6.2 10.1 %legendre.3 = bf16[8,4,2,24,16,128]{5,4,3,2,1,0:T(8,128)(2,1)} custom-call(s32[24]{0:T(128)} %dynamic_slice.21.waves, bf16[16416,128]{1,0:T(8,128)(2,1)} %bitcast.32, bf16[16416,128]{1,0:T(8,128)(2,1)} %bitcast.27, bf16[24,171,256]{2,1,0:T(8,128)(2,1)} %copy.52.leg_ref, f32[171,1]{1,0:T(8,128)} %fusion.28.factor_ref, f32[256,1]{1,0:T(8,128)} %copy.43.quad_ref), custom_call_target="tpu_custom_call" | custom-call | flops 1075838976 | bytes 15747072 | tf_op jit(solution)/shard_map/legendre/pallas_call | solution.py:90
  16.3 7.4 %all-to-all-start = ((bf16[32,2,24,16,128]{4,3,2,1,0:T(8,128)(2,1)}), bf16[32,2,24,16,128]{4,3,2,1,0:T(8,128)(2,1)}, u32[]{:S(2)}, u32[]{:S(2)}) async-start(bf16[32,2,24,16,128]{4,3,2,1,0:T(8,128)(2,1)} %bitcast.31), calls=%async_computation | async-start | bytes 12582912 | tf_op jit(solution)/shard_map/all_to_all | solution.py:427
  23.7 10.1 %legendre.2 = bf16[8,4,2,24,16,128]{5,4,3,2,1,0:T(8,128)(2,1)} custom-call(s32[24]{0:T(128)} %dynamic_slice.21.waves, bf16[16416,128]{1,0:T(8,128)(2,1)} %bitcast.33, bf16[16416,128]{1,0:T(8,128)(2,1)} %bitcast.28, bf16[24,171,256]{2,1,0:T(8,128)(2,1)} %copy.52.leg_ref, f32[171,1]{1,0:T(8,128)} %fusion.28.factor_ref, f32[256,1]{1,0:T(8,128)} %copy.43.quad_ref), custom_call_target="tpu_custom_call" | custom-call | flops 1075838976 | bytes 15747072 | tf_op jit(solution)/shard_map/legendre/pallas_call | solution.py:90
  33.9 129.6 %all-to-all-done = bf16[32,2,24,16,128]{4,3,2,1,0:T(8,128)(2,1)} async-done(((bf16[32,2,24,16,128]{4,3,2,1,0:T(8,128)(2,1)}), bf16[32,2,24,16,128]{4,3,2,1,0:T(8,128)(2,1)}, u32[]{:S(2)}, u32[]{:S(2)}) %all-to-all-start) | async-done | bytes 6291488 | tf_op jit(solution)/shard_map/all_to_all | solution.py:427
  163.5 3.6 all-to-all-start.2
  167.1 0.0 copy-start.2
  167.1 0.0 copy-start.3
  167.1 0.0 copy-start.4
  167.2 1.9 multiply_convert_fusion.1
  169.1 0.8 pad_maximum_fusion.1
  169.9 0.9 copy.49.table_ref
  170.8 1.0 copy.47
  171.8 0.8 copy.48
  172.6 0.0 copy-done.4
  172.6 0.9 copy.46
  173.5 1.0 fusion.22
  174.5 75.7 %columns.3 = (bf16[8,4,24,16,128]{4,3,2,1,0:T(8,128)(2,1)}, f32[1088,512]{1,0:T(8,128)}) custom-call(bf16[8,4,2,24,16,128]{5,4,3,2,1,0:T(8,128)(2,1)} %bitcast.4.state_ref.cot_ref, bf16[8,4,2,24,16,128]{5,4,3,2,1,0:T(8,128)(2,1)} %bitcast.4.state_ref.cot_ref, bf16[512,384]{1,0:T(8,128)(2,1)} %copy.49.table_ref, ...), custom_call_target="tpu_custom_call" | custom-call | flops 30601641984 | bytes 13893632 | tf_op jit(solution)/shard_map/columns/pallas_call | solution.py:349
  250.2 56.6 %all-to-all-done.2 = bf16[32,2,24,16,128]{4,3,2,1,0:T(8,128)(2,1)} async-done(((bf16[32,2,24,16,128]{4,3,2,1,0:T(8,128)(2,1)}), bf16[32,2,24,16,128]{4,3,2,1,0:T(8,128)(2,1)}, u32[]{:S(2)}, u32[]{:S(2)}) %all-to-all-start.2) | async-done | bytes 6291488 | tf_op jit(solution)/shard_map/all_to_all | solution.py:427
  306.9 2.9 all-to-all-start.1
  309.8 38.2 %columns.4 = (bf16[8,4,24,8,128]{4,3,2,1,0:T(8,128)(2,1)}, f32[1088,512]{1,0:T(8,128)}) custom-call(bf16[8,4,2,24,16,128]{5,4,3,2,1,0:T(8,128)(2,1)} %bitcast.15.state_ref.cot_ref, bf16[8,4,2,24,16,128]{5,4,3,2,1,0:T(8,128)(2,1)} %bitcast.15.state_ref.cot_ref, bf16[512,384]{1,0:T(8,128)(2,1)} %copy.49.table_ref, ...), custom_call_target="tpu_custom_call" | custom-call | flops 15300820992 | bytes 9175040 | tf_op jit(solution)/shard_map/columns/pallas_call | solution.py:349
  348.0 38.0 %columns.5 = (bf16[8,4,24,8,128]{4,3,2,1,0:T(8,128)(2,1)}, f32[1088,512]{1,0:T(8,128)}) custom-call(bf16[8,4,2,24,16,128]{5,4,3,2,1,0:T(8,128)(2,1)} %bitcast.15.state_ref.cot_ref, bf16[8,4,2,24,16,128]{5,4,3,2,1,0:T(8,128)(2,1)} %bitcast.15.state_ref.cot_ref, bf16[512,384]{1,0:T(8,128)(2,1)} %copy.49.table_ref, ...), custom_call_target="tpu_custom_call" | custom-call | flops 15300820992 | bytes 9175040 | tf_op jit(solution)/shard_map/columns/pallas_call | solution.py:349
  386.0 0.0 all-to-all-done.1
  386.0 6.1 %all-to-all-start.4 = ((bf16[32,24,8,128]{3,2,1,0:T(8,128)(2,1)}), bf16[32,24,8,128]{3,2,1,0:T(8,128)(2,1)}, u32[]{:S(2)}, u32[]{:S(2)}) async-start(bf16[32,24,8,128]{3,2,1,0:T(8,128)(2,1)} %bitcast.37), calls=%async_computation.4 | async-start | bytes 3145728 | tf_op jit(solution)/shard_map/all_to_all | solution.py:427
  392.2 2.1 dynamic-slice_convert_fusion
  394.3 0.0 collective-permute-start
  394.3 2.3 collective-permute-done
  396.6 1.6 convert_add_fusion
  398.2 0.0 copy-start.1
  398.3 0.9 copy-done.1
  399.2 1.5 collective-permute-start.1
  400.7 14.0 %collective-permute-done.1 = bf16[272,512]{1,0:T(8,128)(2,1)S(1)} collective-permute-done((bf16[272,512]{1,0:T(8,128)(2,1)S(1)}, bf16[272,512]{1,0:T(8,128)(2,1)S(1)}, u32[]{:S(2)}, u32[]{:S(2)}) %collective-permute-start.1) | collective-permute-done | bytes 278560 | tf_op jit(solution)/shard_map/ppermute | solution.py:369
  414.8 1.1 convert_add_fusion.1
  415.9 1.1 collective-permute-start.2
  417.1 5.4 %collective-permute-done.2 = bf16[136,512]{1,0:T(8,128)(2,1)S(1)} collective-permute-done((bf16[136,512]{1,0:T(8,128)(2,1)S(1)}, bf16[136,512]{1,0:T(8,128)(2,1)S(1)}, u32[]{:S(2)}, u32[]{:S(2)}) %collective-permute-start.2) | collective-permute-done | bytes 139296 | tf_op jit(solution)/shard_map/ppermute | solution.py:369
  422.5 0.3 collective-permute-start.3
  422.8 3.0 collective-permute-start.4
  425.8 1.2 collective-permute-start.5
  426.9 9.3 %all-to-all-done.4 = bf16[32,24,8,128]{3,2,1,0:T(8,128)(2,1)} async-done(((bf16[32,24,8,128]{3,2,1,0:T(8,128)(2,1)}), bf16[32,24,8,128]{3,2,1,0:T(8,128)(2,1)}, u32[]{:S(2)}, u32[]{:S(2)}) %all-to-all-start.4) | async-done | bytes 1572896 | tf_op jit(solution)/shard_map/all_to_all | solution.py:427
  436.2 3.4 all-to-all-start.3
  439.7 0.0 collective-permute-done.3
  439.7 0.0 collective-permute-done.4
  439.7 0.0 collective-permute-done.5
  439.7 0.1 add_convert_fusion
  439.8 1.7 collective-permute-start.6
  441.4 13.3 %collective-permute-done.6 = bf16[136,512]{1,0:T(8,128)(2,1)S(1)} collective-permute-done((bf16[136,512]{1,0:T(8,128)(2,1)S(1)}, bf16[136,512]{1,0:T(8,128)(2,1)S(1)}, u32[]{:S(2)}, u32[]{:S(2)}) %collective-permute-start.6) | collective-permute-done | bytes 139296 | tf_op jit(solution)/shard_map/ppermute | solution.py:369
  454.8 3.4 collective-permute-start.7
  458.2 9.4 %collective-permute-done.7 = bf16[272,512]{1,0:T(8,128)(2,1)S(1)} collective-permute-done((bf16[272,512]{1,0:T(8,128)(2,1)S(1)}, bf16[272,512]{1,0:T(8,128)(2,1)S(1)}, u32[]{:S(2)}, u32[]{:S(2)}) %collective-permute-start.7) | collective-permute-done | bytes 278560 | tf_op jit(solution)/shard_map/ppermute | solution.py:369
  467.6 0.1 broadcast_select_fusion.3
  467.8 0.2 collective-permute-start.8
  468.0 1.8 collective-permute-done.8
  469.8 0.2 broadcast_select_fusion.1
  470.0 0.3 convert_multiply_fusion
  470.3 1.0 slice.27
  471.4 0.6 slice.24
  471.9 0.9 slice_bitcast_fusion
  472.8 1.0 copy.53
  473.8 0.6 fusion.32
  474.4 3.1 all-to-all-done.3
  477.5 10.4 %inverse_legendre.1 = f32[16416,128]{1,0:T(8,128)} custom-call(s32[24]{0:T(128)} %dynamic_slice.21.waves, bf16[16416,128]{1,0:T(8,128)(2,1)} %bitcast.29, bf16[24,171,256]{2,1,0:T(8,128)(2,1)} %copy.52.leg_ref, f32[171,1]{1,0:T(8,128)} %fusion.28.factor_ref, bf16[8,4,24,16,128]{4,3,2,1,0:T(8,128)(2,1)} %bitcast.34, ...), custom_call_target="tpu_custom_call" | custom-call | flops 1075838976 | bytes 21000192 | tf_op jit(solution)/shard_map/inverse_legendre/pallas_call | solution.py:151
  (17 shorter events, 0.2 us)
Async XLA Ops:
  0.6 4.1 copy-start.6
  1.3 4.2 copy-start.5
  16.3 147.2 %all-to-all-start = ((bf16[32,2,24,16,128]{4,3,2,1,0:T(8,128)(2,1)}), bf16[32,2,24,16,128]{4,3,2,1,0:T(8,128)(2,1)}, u32[]{:S(2)}, u32[]{:S(2)}) async-start(bf16[32,2,24,16,128]{4,3,2,1,0:T(8,128)(2,1)} %bitcast.31), calls=%async_computation | async-start | bytes 12582912 | tf_op jit(solution)/shard_map/all_to_all | solution.py:427
  163.5 143.4 %all-to-all-start.2 = ((bf16[32,2,24,16,128]{4,3,2,1,0:T(8,128)(2,1)}), bf16[32,2,24,16,128]{4,3,2,1,0:T(8,128)(2,1)}, u32[]{:S(2)}, u32[]{:S(2)}) async-start(bf16[32,2,24,16,128]{4,3,2,1,0:T(8,128)(2,1)} %bitcast.30), calls=%async_computation.2 | async-start | bytes 12582912 | tf_op jit(solution)/shard_map/all_to_all | solution.py:427
  167.1 3.7 copy-start.2
  167.1 4.7 copy-start.3
  167.1 5.5 %copy-start.4 = (bf16[256,512]{1,0:T(8,128)(2,1)S(1)}, bf16[256,512]{1,0:T(8,128)(2,1)}, u32[]{:S(2)}) copy-start(bf16[256,512]{1,0:T(8,128)(2,1)} %w_in_ref.5) | copy-start | bytes 786436
  306.9 79.1 %all-to-all-start.1 = ((bf16[32,24,16,128]{3,2,1,0:T(8,128)(2,1)}), bf16[32,24,16,128]{3,2,1,0:T(8,128)(2,1)S(1)}, u32[]{:S(2)}, u32[]{:S(2)}) async-start(bf16[32,24,16,128]{3,2,1,0:T(8,128)(2,1)} %bitcast.36), calls=%async_computation.1 | async-start | bytes 6291456 | tf_op jit(solution)/shard_map/all_to_all | solution.py:427
  386.0 12.2 %copy-start = (bf16[32,24,16,128]{3,2,1,0:T(8,128)(2,1)}, bf16[32,24,16,128]{3,2,1,0:T(8,128)(2,1)S(1)}, u32[]{:S(2)}) copy-start(bf16[32,24,16,128]{3,2,1,0:T(8,128)(2,1)S(1)} %all-to-all-done.1) | copy-start | bytes 9437188
  386.0 50.2 %all-to-all-start.4 = ((bf16[32,24,8,128]{3,2,1,0:T(8,128)(2,1)}), bf16[32,24,8,128]{3,2,1,0:T(8,128)(2,1)}, u32[]{:S(2)}, u32[]{:S(2)}) async-start(bf16[32,24,8,128]{3,2,1,0:T(8,128)(2,1)} %bitcast.37), calls=%async_computation.4 | async-start | bytes 3145728 | tf_op jit(solution)/shard_map/all_to_all | solution.py:427
  394.3 2.3 collective-permute-start
  398.2 1.0 copy-start.1
  399.2 15.5 %collective-permute-start.1 = (bf16[272,512]{1,0:T(8,128)(2,1)S(1)}, bf16[272,512]{1,0:T(8,128)(2,1)S(1)}, u32[]{:S(2)}, u32[]{:S(2)}) collective-permute-start(bf16[272,512]{1,0:T(8,128)(2,1)S(1)} %dynamic-slice_convert_fusion.1), channel_id=1, source_target_pairs={{0,2},{1,3},{2,0},{3,1},{4,6},{5,7},{6,4},{7,5},{8,10},{9,11},{10,... | collective-permute-start | bytes 835592 | tf_op jit(solution)/shard_map/ppermute | solution.py:369
  415.9 6.5 %collective-permute-start.2 = (bf16[136,512]{1,0:T(8,128)(2,1)S(1)}, bf16[136,512]{1,0:T(8,128)(2,1)S(1)}, u32[]{:S(2)}, u32[]{:S(2)}) collective-permute-start(bf16[136,512]{1,0:T(8,128)(2,1)S(1)} %dynamic-slice_convert_fusion.2), channel_id=1, source_target_pairs={{0,4},{4,0},{8,12},{12,8},{16,20},{20,16},{24,28},{28,24},{1,5},{5... | collective-permute-start | bytes 417800 | tf_op jit(solution)/shard_map/ppermute | solution.py:369
  422.5 17.2 %collective-permute-start.3 = (bf16[136,512]{1,0:T(8,128)(2,1)S(1)}, bf16[136,512]{1,0:T(8,128)(2,1)S(1)}, u32[]{:S(2)}, u32[]{:S(2)}) collective-permute-start(bf16[136,512]{1,0:T(8,128)(2,1)S(1)} %add_convert_fusion.1), channel_id=1, source_target_pairs={{0,8},{4,12},{8,0},{12,4},{16,24},{20,28},{24,16},{28,20},{1,9},{5... | collective-permute-start | bytes 417800 | tf_op jit(solution)/shard_map/ppermute | solution.py:369
  422.8 16.9 %collective-permute-start.4 = (bf16[136,512]{1,0:T(8,128)(2,1)S(1)}, bf16[136,512]{1,0:T(8,128)(2,1)S(1)}, u32[]{:S(2)}, u32[]{:S(2)}) collective-permute-start(bf16[136,512]{1,0:T(8,128)(2,1)S(1)} %add_convert_fusion.1), channel_id=1, source_target_pairs={{0,16},{4,20},{8,24},{12,28},{16,0},{20,4},{24,8},{28,12},{1,17},{... | collective-permute-start | bytes 417800 | tf_op jit(solution)/shard_map/ppermute | solution.py:369
  425.8 13.9 %collective-permute-start.5 = (bf16[136,512]{1,0:T(8,128)(2,1)S(1)}, bf16[136,512]{1,0:T(8,128)(2,1)S(1)}, u32[]{:S(2)}, u32[]{:S(2)}) collective-permute-start(bf16[136,512]{1,0:T(8,128)(2,1)S(1)} %add_convert_fusion.1), channel_id=1, source_target_pairs={{0,24},{4,28},{8,16},{12,20},{16,8},{20,12},{24,0},{28,4},{1,25},{... | collective-permute-start | bytes 417800 | tf_op jit(solution)/shard_map/ppermute | solution.py:369
  436.2 41.3 %all-to-all-start.3 = ((bf16[32,24,8,128]{3,2,1,0:T(8,128)(2,1)}), bf16[32,24,8,128]{3,2,1,0:T(8,128)(2,1)}, u32[]{:S(2)}, u32[]{:S(2)}) async-start(bf16[32,24,8,128]{3,2,1,0:T(8,128)(2,1)} %bitcast.16), calls=%async_computation.3 | async-start | bytes 3145728 | tf_op jit(solution)/shard_map/all_to_all | solution.py:427
  439.8 15.0 %collective-permute-start.6 = (bf16[136,512]{1,0:T(8,128)(2,1)S(1)}, bf16[136,512]{1,0:T(8,128)(2,1)S(1)}, u32[]{:S(2)}, u32[]{:S(2)}) collective-permute-start(bf16[136,512]{1,0:T(8,128)(2,1)S(1)} %add_convert_fusion), channel_id=1, source_target_pairs={{0,4},{4,0},{8,12},{12,8},{16,20},{20,16},{24,28},{28,24},{1,5},{5... | collective-permute-start | bytes 417800 | tf_op jit(solution)/shard_map/ppermute | solution.py:369
  454.8 12.8 %collective-permute-start.7 = (bf16[272,512]{1,0:T(8,128)(2,1)S(1)}, bf16[272,512]{1,0:T(8,128)(2,1)S(1)}, u32[]{:S(2)}, u32[]{:S(2)}) collective-permute-start(bf16[272,512]{1,0:T(8,128)(2,1)S(1)} %pad_maximum_fusion.2), channel_id=1, source_target_pairs={{0,2},{1,3},{2,0},{3,1},{4,6},{5,7},{6,4},{7,5},{8,10},{9,11},{10,... | collective-permute-start | bytes 835592 | tf_op jit(solution)/shard_map/ppermute | solution.py:369
  467.8 2.0 collective-permute-start.8

commit v4 on v3

--- a/solution.py
+++ b/solution.py
@@ -82,7 +82,7 @@
     slots, degrees, nlat = legendre_table.shape
     lanes = spec.shape[1]
     members = spec.shape[0] // (slots * degrees)
-    pair = 4 if slots % 4 == 0 else 2
+    pair = 8 if slots % 8 == 0 else 2
     span = nlat // chunks
     rows = span // lat_count
     block = pair * degrees * members
@@ -146,7 +146,7 @@
     slots, degrees, nlat = legendre_table.shape
     lanes = packed.shape[1]
     members = packed.shape[0] // (slots * degrees)
-    pair = 4 if slots % 4 == 0 else 2
+    pair = 8 if slots % 8 == 0 else 2
     block = pair * degrees * members
     return pl.pallas_call(
         functools.partial(inverse_kernel, pair, members, degrees, counts),
@@ -310,7 +310,7 @@
     slots = lat_count * slots_here
     weight_in, bias_in, weight_mid, bias_mid, weight_out = weights
     channels, hidden = weight_in.shape
-    block = NLON // 2
+    block = NLON
     grad_rows = -(-(2 * channels + hidden + 3) // 64) * 64
     operands = [
         table,
@@ -384,8 +384,8 @@
         kept = lax.dynamic_slice_in_dim(total, side * size, size)
         total = kept + swap(sent, axis, bit).astype(F32)
     part = total.astype(BF16)
-    one, two, three = (swap(part, "lat", k * top).astype(F32) for k in (1, 2, 3))
-    part = ((part.astype(F32) + one) + (two + three)).astype(BF16)
+    for k in (1, 2):
+        part = (part.astype(F32) + swap(part, "lat", k * top).astype(F32)).astype(BF16)
     for axis, bit in reversed(steps):
         side = (lax.axis_index(axis) // bit) % 2
         other = swap(part, axis, bit)

time: 489 us -> 478 us (0.978)
  Pallas kernels: 183 us -> 156 us
  waiting for transfers between devices: 245 us -> 267 us
  starting transfers between devices: 35.9 us -> 29.9 us
    pallas_call x3, Pallas kernels: 152 us -> 125 us  [column_grads(): pl.pallas_call(functools.partial(column_kernel, rows, block, before is no...]
    all_to_all x5, waiting for transfers between devices: 199 us -> 213 us  [exchange(): x = lax.all_to_all(x, axes, split_axis=0, concat_axis=0, tiled=True)]
    ppermute x9 -> x8, waiting for transfers between devices: 46.2 us -> 54.2 us  [swap(): lax.ppermute(x, axis, [(i, i ^ bits) for i in range(lax.axis_size(axis))])]
    ppermute x9 -> x8, starting transfers between devices: 12.4 us -> 8.33 us  [swap(): lax.ppermute(x, axis, [(i, i ^ bits) for i in range(lax.axis_size(axis))])]
  transfers between devices with their start and end apart: 14 -> 13, of which waited for: 10 -> 12; matrix products, arithmetic and copies ran while one was open for 4% -> 4% of each run, Pallas kernels for 33% -> 28%
where the time goes in v4:
time: 478 us; the launch traced here: 477 us
  waiting for transfers between devices  267 us (56%)
  Pallas kernels  156 us (33%)
  starting transfers between devices  29.9 us (6%)
  local copies, waits for them, and re-layouts  15.6 us (3%)
  other arithmetic  7.87 us (2%)
    all_to_all x5, waiting for transfers between devices, exchange(): x = lax.all_to_all(x, axes, split_axis=0, concat_axis=0, tiled=True)  213 us
    pallas_call x3, Pallas kernels, column_grads(): pl.pallas_call(functools.partial(column_kernel, rows, block, before is no...  125 us
    ppermute x8, waiting for transfers between devices, swap(): lax.ppermute(x, axis, [(i, i ^ bits) for i in range(lax.axis_size(axis))])  54.2 us
    all_to_all x5, starting transfers between devices, exchange(): x = lax.all_to_all(x, axes, split_axis=0, concat_axis=0, tiled=True)  21.6 us
    pallas_call x2, Pallas kernels, legendre(): pl.pallas_call(functools.partial(legendre_kernel, pair, members, degrees)...  20.6 us
    pallas_call x1, Pallas kernels, inverse_legendre(): pl.pallas_call(functools.partial(inverse_kernel, pair, members, degrees,...  10.6 us
  transfers between devices with their start and end apart: 13, of which 12 were waited for; matrix products, arithmetic and copies ran while one was open for 4% of the time, Pallas kernels for 28%

profile of v4, /device:TPU:0, one launch (start us, length us, event | category | flops | bytes accessed | tf_op | source)
XLA Modules:
  0.0 477.3 jit_solution(11809706409994781471)
XLA Ops:
  0.6 0.0 copy-start.6
  0.6 0.7 fusion.28.factor_ref
  1.3 3.4 copy.52.leg_ref
  4.7 0.0 copy-done.6
  4.7 0.8 copy.43.quad_ref
  5.5 0.0 copy-done.5
  5.5 0.6 dynamic_slice.21.waves
  6.1 10.3 %legendre.3 = bf16[8,4,2,24,16,128]{5,4,3,2,1,0:T(8,128)(2,1)} custom-call(s32[24]{0:T(128)} %dynamic_slice.21.waves, bf16[16416,128]{1,0:T(8,128)(2,1)} %bitcast.32, bf16[16416,128]{1,0:T(8,128)(2,1)} %bitcast.27, bf16[24,171,256]{2,1,0:T(8,128)(2,1)} %copy.52.leg_ref, f32[171,1]{1,0:T(8,128)} %fusion.28.factor_ref, f32[256,1]{1,0:T(8,128)} %copy.43.quad_ref), custom_call_target="tpu_custom_call" | custom-call | flops 1075838976 | bytes 15747072 | tf_op jit(solution)/shard_map/legendre/pallas_call | solution.py:90
  16.4 7.4 %all-to-all-start = ((bf16[32,2,24,16,128]{4,3,2,1,0:T(8,128)(2,1)}), bf16[32,2,24,16,128]{4,3,2,1,0:T(8,128)(2,1)}, u32[]{:S(2)}, u32[]{:S(2)}) async-start(bf16[32,2,24,16,128]{4,3,2,1,0:T(8,128)(2,1)} %bitcast.31), calls=%async_computation | async-start | bytes 12582912 | tf_op jit(solution)/shard_map/all_to_all | solution.py:427
  23.8 10.3 %legendre.2 = bf16[8,4,2,24,16,128]{5,4,3,2,1,0:T(8,128)(2,1)} custom-call(s32[24]{0:T(128)} %dynamic_slice.21.waves, bf16[16416,128]{1,0:T(8,128)(2,1)} %bitcast.33, bf16[16416,128]{1,0:T(8,128)(2,1)} %bitcast.28, bf16[24,171,256]{2,1,0:T(8,128)(2,1)} %copy.52.leg_ref, f32[171,1]{1,0:T(8,128)} %fusion.28.factor_ref, f32[256,1]{1,0:T(8,128)} %copy.43.quad_ref), custom_call_target="tpu_custom_call" | custom-call | flops 1075838976 | bytes 15747072 | tf_op jit(solution)/shard_map/legendre/pallas_call | solution.py:90
  34.2 129.4 %all-to-all-done = bf16[32,2,24,16,128]{4,3,2,1,0:T(8,128)(2,1)} async-done(((bf16[32,2,24,16,128]{4,3,2,1,0:T(8,128)(2,1)}), bf16[32,2,24,16,128]{4,3,2,1,0:T(8,128)(2,1)}, u32[]{:S(2)}, u32[]{:S(2)}) %all-to-all-start) | async-done | bytes 6291488 | tf_op jit(solution)/shard_map/all_to_all | solution.py:427
  163.6 3.6 all-to-all-start.2
  167.2 0.0 copy-start.2
  167.2 0.0 copy-start.3
  167.2 0.0 copy-start.4
  167.2 1.9 multiply_convert_fusion.1
  169.1 0.8 pad_maximum_fusion.1
  169.9 0.9 copy.49.table_ref
  170.9 0.0 copy-done.2
  170.9 1.0 copy.47
  171.9 0.8 copy.48
  172.7 0.9 copy.46
  173.6 1.0 fusion.22
  174.6 61.5 %columns.3 = (bf16[8,4,24,16,128]{4,3,2,1,0:T(8,128)(2,1)}, f32[1088,512]{1,0:T(8,128)}) custom-call(bf16[8,4,2,24,16,128]{5,4,3,2,1,0:T(8,128)(2,1)} %bitcast.4.state_ref.cot_ref, bf16[8,4,2,24,16,128]{5,4,3,2,1,0:T(8,128)(2,1)} %bitcast.4.state_ref.cot_ref, bf16[512,384]{1,0:T(8,128)(2,1)} %copy.49.table_ref, ...), custom_call_target="tpu_custom_call" | custom-call | flops 30601641984 | bytes 13893632 | tf_op jit(solution)/shard_map/columns/pallas_call | solution.py:349
  236.1 70.8 %all-to-all-done.2 = bf16[32,2,24,16,128]{4,3,2,1,0:T(8,128)(2,1)} async-done(((bf16[32,2,24,16,128]{4,3,2,1,0:T(8,128)(2,1)}), bf16[32,2,24,16,128]{4,3,2,1,0:T(8,128)(2,1)}, u32[]{:S(2)}, u32[]{:S(2)}) %all-to-all-start.2) | async-done | bytes 6291488 | tf_op jit(solution)/shard_map/all_to_all | solution.py:427
  306.9 3.1 all-to-all-start.1
  310.0 31.6 %columns.4 = (bf16[8,4,24,8,128]{4,3,2,1,0:T(8,128)(2,1)}, f32[1088,512]{1,0:T(8,128)}) custom-call(bf16[8,4,2,24,16,128]{5,4,3,2,1,0:T(8,128)(2,1)} %bitcast.15.state_ref.cot_ref, bf16[8,4,2,24,16,128]{5,4,3,2,1,0:T(8,128)(2,1)} %bitcast.15.state_ref.cot_ref, bf16[512,384]{1,0:T(8,128)(2,1)} %copy.49.table_ref, ...), custom_call_target="tpu_custom_call" | custom-call | flops 15300820992 | bytes 9175040 | tf_op jit(solution)/shard_map/columns/pallas_call | solution.py:349
  341.7 31.6 %columns.5 = (bf16[8,4,24,8,128]{4,3,2,1,0:T(8,128)(2,1)}, f32[1088,512]{1,0:T(8,128)}) custom-call(bf16[8,4,2,24,16,128]{5,4,3,2,1,0:T(8,128)(2,1)} %bitcast.15.state_ref.cot_ref, bf16[8,4,2,24,16,128]{5,4,3,2,1,0:T(8,128)(2,1)} %bitcast.15.state_ref.cot_ref, bf16[512,384]{1,0:T(8,128)(2,1)} %copy.49.table_ref, ...), custom_call_target="tpu_custom_call" | custom-call | flops 15300820992 | bytes 9175040 | tf_op jit(solution)/shard_map/columns/pallas_call | solution.py:349
  373.3 8.0 %all-to-all-done.1 = bf16[32,24,16,128]{3,2,1,0:T(8,128)(2,1)S(1)} async-done(((bf16[32,24,16,128]{3,2,1,0:T(8,128)(2,1)}), bf16[32,24,16,128]{3,2,1,0:T(8,128)(2,1)S(1)}, u32[]{:S(2)}, u32[]{:S(2)}) %all-to-all-start.1) | async-done | bytes 3145760 | tf_op jit(solution)/shard_map/all_to_all | solution.py:427
  381.3 4.0 all-to-all-start.4
  385.4 2.1 dynamic-slice_convert_fusion
  387.5 0.2 collective-permute-start
  387.7 2.1 collective-permute-done
  389.8 1.6 convert_add_fusion
  391.4 0.0 copy-done
  391.4 0.0 copy-start.1
  391.5 0.9 copy-done.1
  392.4 1.7 collective-permute-start.1
  394.1 14.0 %collective-permute-done.1 = bf16[272,512]{1,0:T(8,128)(2,1)S(1)} collective-permute-done((bf16[272,512]{1,0:T(8,128)(2,1)S(1)}, bf16[272,512]{1,0:T(8,128)(2,1)S(1)}, u32[]{:S(2)}, u32[]{:S(2)}) %collective-permute-start.1) | collective-permute-done | bytes 278560 | tf_op jit(solution)/shard_map/ppermute | solution.py:369
  408.1 1.1 convert_add_fusion.1
  409.3 1.1 collective-permute-start.2
  410.4 5.4 %collective-permute-done.2 = bf16[136,512]{1,0:T(8,128)(2,1)S(1)} collective-permute-done((bf16[136,512]{1,0:T(8,128)(2,1)S(1)}, bf16[136,512]{1,0:T(8,128)(2,1)S(1)}, u32[]{:S(2)}, u32[]{:S(2)}) %collective-permute-start.2) | collective-permute-done | bytes 139296 | tf_op jit(solution)/shard_map/ppermute | solution.py:369
  415.8 0.3 collective-permute-start.3
  416.1 8.0 %collective-permute-done.3 = bf16[136,512]{1,0:T(8,128)(2,1)S(1)} collective-permute-done((bf16[136,512]{1,0:T(8,128)(2,1)S(1)}, bf16[136,512]{1,0:T(8,128)(2,1)S(1)}, u32[]{:S(2)}, u32[]{:S(2)}) %collective-permute-start.3) | collective-permute-done | bytes 139296 | tf_op jit(solution)/shard_map/ppermute | solution.py:369
  424.2 0.1 collective-permute-start.4
  424.3 0.0 all-to-all-done.4
  424.3 3.4 all-to-all-start.3
  427.8 4.9 %collective-permute-done.4 = bf16[136,512]{1,0:T(8,128)(2,1)S(1)} collective-permute-done((bf16[136,512]{1,0:T(8,128)(2,1)S(1)}, bf16[136,512]{1,0:T(8,128)(2,1)S(1)}, u32[]{:S(2)}, u32[]{:S(2)}) %collective-permute-start.4) | collective-permute-done | bytes 139296 | tf_op jit(solution)/shard_map/ppermute | solution.py:369
  432.7 0.1 collective-permute-start.5
  432.8 8.5 %collective-permute-done.5 = bf16[136,512]{1,0:T(8,128)(2,1)S(1)} collective-permute-done((bf16[136,512]{1,0:T(8,128)(2,1)S(1)}, bf16[136,512]{1,0:T(8,128)(2,1)S(1)}, u32[]{:S(2)}, u32[]{:S(2)}) %collective-permute-start.5) | collective-permute-done | bytes 139296 | tf_op jit(solution)/shard_map/ppermute | solution.py:369
  441.4 4.7 collective-permute-start.6
  446.1 9.4 %collective-permute-done.6 = bf16[272,512]{1,0:T(8,128)(2,1)S(1)} collective-permute-done((bf16[272,512]{1,0:T(8,128)(2,1)S(1)}, bf16[272,512]{1,0:T(8,128)(2,1)S(1)}, u32[]{:S(2)}, u32[]{:S(2)}) %collective-permute-start.6) | collective-permute-done | bytes 278560 | tf_op jit(solution)/shard_map/ppermute | solution.py:369
  455.4 0.1 broadcast_select_fusion.3
  455.6 0.1 collective-permute-start.7
  455.7 1.9 collective-permute-done.7
  457.6 0.2 broadcast_select_fusion.1
  457.8 0.3 convert_multiply_fusion
  458.1 1.0 slice.27
  459.1 0.6 slice.24
  459.7 0.9 slice_bitcast_fusion
  460.6 1.0 copy.53
  461.6 0.6 fusion.32
  462.2 4.5 all-to-all-done.3
  466.7 10.6 %inverse_legendre.1 = f32[16416,128]{1,0:T(8,128)} custom-call(s32[24]{0:T(128)} %dynamic_slice.21.waves, bf16[16416,128]{1,0:T(8,128)(2,1)} %bitcast.29, bf16[24,171,256]{2,1,0:T(8,128)(2,1)} %copy.52.leg_ref, f32[171,1]{1,0:T(8,128)} %fusion.28.factor_ref, bf16[8,4,24,16,128]{4,3,2,1,0:T(8,128)(2,1)} %bitcast.34, ...), custom_call_target="tpu_custom_call" | custom-call | flops 1075838976 | bytes 21000192 | tf_op jit(solution)/shard_map/inverse_legendre/pallas_call | solution.py:151
  (16 shorter events, 0.3 us)
Async XLA Ops:
  0.6 4.1 copy-start.6
  1.3 4.2 copy-start.5
  16.4 147.2 %all-to-all-start = ((bf16[32,2,24,16,128]{4,3,2,1,0:T(8,128)(2,1)}), bf16[32,2,24,16,128]{4,3,2,1,0:T(8,128)(2,1)}, u32[]{:S(2)}, u32[]{:S(2)}) async-start(bf16[32,2,24,16,128]{4,3,2,1,0:T(8,128)(2,1)} %bitcast.31), calls=%async_computation | async-start | bytes 12582912 | tf_op jit(solution)/shard_map/all_to_all | solution.py:427
  163.6 143.4 %all-to-all-start.2 = ((bf16[32,2,24,16,128]{4,3,2,1,0:T(8,128)(2,1)}), bf16[32,2,24,16,128]{4,3,2,1,0:T(8,128)(2,1)}, u32[]{:S(2)}, u32[]{:S(2)}) async-start(bf16[32,2,24,16,128]{4,3,2,1,0:T(8,128)(2,1)} %bitcast.30), calls=%async_computation.2 | async-start | bytes 12582912 | tf_op jit(solution)/shard_map/all_to_all | solution.py:427
  167.2 3.7 copy-start.2
  167.2 4.7 copy-start.3
  167.2 5.5 %copy-start.4 = (bf16[256,512]{1,0:T(8,128)(2,1)S(1)}, bf16[256,512]{1,0:T(8,128)(2,1)}, u32[]{:S(2)}) copy-start(bf16[256,512]{1,0:T(8,128)(2,1)} %w_in_ref.5) | copy-start | bytes 786436
  306.9 74.4 %all-to-all-start.1 = ((bf16[32,24,16,128]{3,2,1,0:T(8,128)(2,1)}), bf16[32,24,16,128]{3,2,1,0:T(8,128)(2,1)S(1)}, u32[]{:S(2)}, u32[]{:S(2)}) async-start(bf16[32,24,16,128]{3,2,1,0:T(8,128)(2,1)} %bitcast.36), calls=%async_computation.1 | async-start | bytes 6291456 | tf_op jit(solution)/shard_map/all_to_all | solution.py:427
  381.3 10.1 %copy-start = (bf16[32,24,16,128]{3,2,1,0:T(8,128)(2,1)}, bf16[32,24,16,128]{3,2,1,0:T(8,128)(2,1)S(1)}, u32[]{:S(2)}) copy-start(bf16[32,24,16,128]{3,2,1,0:T(8,128)(2,1)S(1)} %all-to-all-done.1) | copy-start | bytes 9437188
  381.3 43.0 %all-to-all-start.4 = ((bf16[32,24,8,128]{3,2,1,0:T(8,128)(2,1)}), bf16[32,24,8,128]{3,2,1,0:T(8,128)(2,1)}, u32[]{:S(2)}, u32[]{:S(2)}) async-start(bf16[32,24,8,128]{3,2,1,0:T(8,128)(2,1)} %bitcast.37), calls=%async_computation.4 | async-start | bytes 3145728 | tf_op jit(solution)/shard_map/all_to_all | solution.py:427
  387.5 2.3 collective-permute-start
  391.4 1.0 copy-start.1
  392.4 15.7 %collective-permute-start.1 = (bf16[272,512]{1,0:T(8,128)(2,1)S(1)}, bf16[272,512]{1,0:T(8,128)(2,1)S(1)}, u32[]{:S(2)}, u32[]{:S(2)}) collective-permute-start(bf16[272,512]{1,0:T(8,128)(2,1)S(1)} %dynamic-slice_convert_fusion.1), channel_id=1, source_target_pairs={{0,2},{1,3},{2,0},{3,1},{4,6},{5,7},{6,4},{7,5},{8,10},{9,11},{10,... | collective-permute-start | bytes 835592 | tf_op jit(solution)/shard_map/ppermute | solution.py:369
  409.3 6.5 %collective-permute-start.2 = (bf16[136,512]{1,0:T(8,128)(2,1)S(1)}, bf16[136,512]{1,0:T(8,128)(2,1)S(1)}, u32[]{:S(2)}, u32[]{:S(2)}) collective-permute-start(bf16[136,512]{1,0:T(8,128)(2,1)S(1)} %dynamic-slice_convert_fusion.2), channel_id=1, source_target_pairs={{0,4},{4,0},{8,12},{12,8},{16,20},{20,16},{24,28},{28,24},{1,5},{5... | collective-permute-start | bytes 417800 | tf_op jit(solution)/shard_map/ppermute | solution.py:369
  415.8 8.4 %collective-permute-start.3 = (bf16[136,512]{1,0:T(8,128)(2,1)S(1)}, bf16[136,512]{1,0:T(8,128)(2,1)S(1)}, u32[]{:S(2)}, u32[]{:S(2)}) collective-permute-start(bf16[136,512]{1,0:T(8,128)(2,1)S(1)} %add_convert_fusion.2), channel_id=1, source_target_pairs={{0,8},{4,12},{8,0},{12,4},{16,24},{20,28},{24,16},{28,20},{1,9},{5... | collective-permute-start | bytes 417800 | tf_op jit(solution)/shard_map/ppermute | solution.py:369
  424.2 8.4 %collective-permute-start.4 = (bf16[136,512]{1,0:T(8,128)(2,1)S(1)}, bf16[136,512]{1,0:T(8,128)(2,1)S(1)}, u32[]{:S(2)}, u32[]{:S(2)}) collective-permute-start(bf16[136,512]{1,0:T(8,128)(2,1)S(1)} %add_convert_fusion.1), channel_id=1, source_target_pairs={{0,16},{4,20},{8,24},{12,28},{16,0},{20,4},{24,8},{28,12},{1,17},{... | collective-permute-start | bytes 417800 | tf_op jit(solution)/shard_map/ppermute | solution.py:369
  424.3 42.4 %all-to-all-start.3 = ((bf16[32,24,8,128]{3,2,1,0:T(8,128)(2,1)}), bf16[32,24,8,128]{3,2,1,0:T(8,128)(2,1)}, u32[]{:S(2)}, u32[]{:S(2)}) async-start(bf16[32,24,8,128]{3,2,1,0:T(8,128)(2,1)} %bitcast.16), calls=%async_computation.3 | async-start | bytes 3145728 | tf_op jit(solution)/shard_map/all_to_all | solution.py:427
  432.7 8.6 %collective-permute-start.5 = (bf16[136,512]{1,0:T(8,128)(2,1)S(1)}, bf16[136,512]{1,0:T(8,128)(2,1)S(1)}, u32[]{:S(2)}, u32[]{:S(2)}) collective-permute-start(bf16[136,512]{1,0:T(8,128)(2,1)S(1)} %add_convert_fusion), channel_id=1, source_target_pairs={{0,4},{4,0},{8,12},{12,8},{16,20},{20,16},{24,28},{28,24},{1,5},{5... | collective-permute-start | bytes 417800 | tf_op jit(solution)/shard_map/ppermute | solution.py:369
  441.4 14.0 %collective-permute-start.6 = (bf16[272,512]{1,0:T(8,128)(2,1)S(1)}, bf16[272,512]{1,0:T(8,128)(2,1)S(1)}, u32[]{:S(2)}, u32[]{:S(2)}) collective-permute-start(bf16[272,512]{1,0:T(8,128)(2,1)S(1)} %pad_maximum_fusion.2), channel_id=1, source_target_pairs={{0,2},{1,3},{2,0},{3,1},{4,6},{5,7},{6,4},{7,5},{8,10},{9,11},{10,... | collective-permute-start | bytes 835592 | tf_op jit(solution)/shard_map/ppermute | solution.py:369
  455.6 2.0 collective-permute-start.7

commit v5 on v4

--- a/solution.py
+++ b/solution.py
@@ -50,17 +50,38 @@
 
 
 def legendre_kernel(
-    pair, members, degrees, waves, x_ref, y_ref, leg_ref, factor_ref, quad_ref, out_ref, x_wide, y_wide
+    pair,
+    members,
+    degrees,
+    swapped,
+    waves,
+    x_ref,
+    y_ref,
+    leg_ref,
+    factor_ref,
+    quad_ref,
+    out_ref,
+    x_wide,
+    y_wide,
+    *leg_wide,
 ):
     step = pl.program_id(0)
     x_wide[...] = x_ref[...].astype(F32)
     y_wide[...] = y_ref[...].astype(F32)
     lat_count, _, _, _, rows, lanes = out_ref.shape
+    span = leg_ref.shape[2]
+    if swapped:
+        (leg_wide,) = leg_wide
+        leg_wide[...] = leg_ref[...].astype(F32).reshape(degrees * pair, span)
     for k in range(pair):
         m = waves[step * pair + k]
-        degree = lax.broadcasted_iota(jnp.int32, leg_ref.shape[1:], 0)
+        degree = lax.broadcasted_iota(jnp.int32, (degrees, span), 0)
         living = (degree >= m) & (m < WAVES)
-        basis = jnp.where(living, leg_ref[k].astype(F32), 0.0).astype(BF16)
+        if swapped:
+            values = leg_wide[pl.ds(k, degrees, stride=pair), :]
+        else:
+            values = leg_ref[k].astype(F32)
+        basis = jnp.where(living, values, 0.0).astype(BF16)
         for is_cot, wide in enumerate((x_wide, y_wide)):
             parts = []
             for e in range(members):
@@ -87,8 +108,15 @@
     rows = span // lat_count
     block = pair * degrees * members
     packed = pl.BlockSpec((block, lanes), lambda i, w: (i, 0))
+    swapped = chunk == 0 and pair == 8 and span == 128
+    scratch = [pltpu.VMEM((block, lanes), F32)] * 2
+    table_spec = pl.BlockSpec((pair, degrees, span), lambda i, w: (i, 0, chunk))
+    if swapped:
+        legendre_table = jnp.transpose(legendre_table, (1, 0, 2))
+        table_spec = pl.BlockSpec((degrees, pair, span), lambda i, w: (0, i, chunk))
+        scratch.append(pltpu.VMEM((degrees * pair, span), F32))
     return pl.pallas_call(
-        functools.partial(legendre_kernel, pair, members, degrees),
+        functools.partial(legendre_kernel, pair, members, degrees, swapped),
         out_shape=jax.ShapeDtypeStruct((lat_count, members, 2, slots, rows, lanes), BF16),
         grid_spec=pltpu.PrefetchScalarGridSpec(
             num_scalar_prefetch=1,
@@ -96,14 +124,14 @@
             in_specs=[
                 packed,
                 packed,
-                pl.BlockSpec((pair, degrees, span), lambda i, w: (i, 0, chunk)),
+                table_spec,
                 pl.BlockSpec((degrees, 1), lambda i, w: (0, 0)),
                 pl.BlockSpec((span, 1), lambda i, w: (chunk, 0)),
             ],
             out_specs=pl.BlockSpec(
                 (lat_count, members, 2, pair, rows, lanes), lambda i, w: (0, 0, 0, i, 0, 0)
             ),
-            scratch_shapes=[pltpu.VMEM((block, lanes), F32)] * 2,
+            scratch_shapes=scratch,
         ),
         compiler_params=pltpu.CompilerParams(
             dimension_semantics=("arbitrary",), vmem_limit_bytes=60 << 20

time: 478 us -> 476 us (level)
  no operation moved by 1% of the time
where the time goes in v5:
time: 476 us; the launch traced here: 475 us
  waiting for transfers between devices  265 us (56%)
  Pallas kernels  156 us (33%)
  starting transfers between devices  30.1 us (6%)
  local copies, waits for them, and re-layouts  15.3 us (3%)
  other arithmetic  7.87 us (2%)
    all_to_all x5, waiting for transfers between devices, exchange(): x = lax.all_to_all(x, axes, split_axis=0, concat_axis=0, tiled=True)  211 us
    pallas_call x3, Pallas kernels, column_grads(): pl.pallas_call(functools.partial(column_kernel, rows, block, before is no...  125 us
    ppermute x8, waiting for transfers between devices, swap(): lax.ppermute(x, axis, [(i, i ^ bits) for i in range(lax.axis_size(axis))])  54.2 us
    all_to_all x5, starting transfers between devices, exchange(): x = lax.all_to_all(x, axes, split_axis=0, concat_axis=0, tiled=True)  21.7 us
    pallas_call x2, Pallas kernels, legendre(): pl.pallas_call(functools.partial(legendre_kernel, pair, members, degrees,...  20.7 us
    pallas_call x1, Pallas kernels, inverse_legendre(): pl.pallas_call(functools.partial(inverse_kernel, pair, members, degrees,...  10.6 us
  transfers between devices with their start and end apart: 13, of which 12 were waited for; matrix products, arithmetic and copies ran while one was open for 4% of the time, Pallas kernels for 28%

profile of v5, /device:TPU:0, one launch (start us, length us, event | category | flops | bytes accessed | tf_op | source)
XLA Modules:
  0.0 475.4 jit_solution(17062624228698897400)
XLA Ops:
  0.6 0.7 fusion.28.factor_ref
  1.3 1.5 copy.41.quad_ref
  2.8 1.2 dynamic_slice.21.waves
  4.0 10.4 %legendre.3 = bf16[8,4,2,24,16,128]{5,4,3,2,1,0:T(8,128)(2,1)} custom-call(s32[24]{0:T(128)} %dynamic_slice.21.waves, bf16[16416,128]{1,0:T(8,128)(2,1)} %bitcast.33, bf16[16416,128]{1,0:T(8,128)(2,1)} %bitcast.28, bf16[171,24,256]{2,1,0:T(8,128)(2,1)} %bitcast.36, f32[171,1]{1,0:T(8,128)} %fusion.28.factor_ref, f32[256,1]{1,0:T(8,128)} %copy.41.quad_ref), custom_call_target="tpu_custom_call" | custom-call | flops 1075838976 | bytes 15747072 | tf_op jit(solution)/shard_map/legendre/pallas_call | solution.py:118
  14.4 7.4 %all-to-all-start = ((bf16[32,2,24,16,128]{4,3,2,1,0:T(8,128)(2,1)}), bf16[32,2,24,16,128]{4,3,2,1,0:T(8,128)(2,1)}, u32[]{:S(2)}, u32[]{:S(2)}) async-start(bf16[32,2,24,16,128]{4,3,2,1,0:T(8,128)(2,1)} %bitcast.32), calls=%async_computation | async-start | bytes 12582912 | tf_op jit(solution)/shard_map/all_to_all | solution.py:455
  21.8 0.0 copy-done.1
  21.8 1.8 copy.49.leg_ref
  23.6 10.3 %legendre.2 = bf16[8,4,2,24,16,128]{5,4,3,2,1,0:T(8,128)(2,1)} custom-call(s32[24]{0:T(128)} %dynamic_slice.21.waves, bf16[16416,128]{1,0:T(8,128)(2,1)} %bitcast.34, bf16[16416,128]{1,0:T(8,128)(2,1)} %bitcast.29, bf16[24,171,256]{2,1,0:T(8,128)(2,1)} %copy.49.leg_ref, f32[171,1]{1,0:T(8,128)} %fusion.28.factor_ref, f32[256,1]{1,0:T(8,128)} %copy.41.quad_ref), custom_call_target="tpu_custom_call" | custom-call | flops 1075838976 | bytes 15747072 | tf_op jit(solution)/shard_map/legendre/pallas_call | solution.py:118
  34.0 127.6 %all-to-all-done = bf16[32,2,24,16,128]{4,3,2,1,0:T(8,128)(2,1)} async-done(((bf16[32,2,24,16,128]{4,3,2,1,0:T(8,128)(2,1)}), bf16[32,2,24,16,128]{4,3,2,1,0:T(8,128)(2,1)}, u32[]{:S(2)}, u32[]{:S(2)}) %all-to-all-start) | async-done | bytes 6291488 | tf_op jit(solution)/shard_map/all_to_all | solution.py:455
  161.6 3.7 all-to-all-start.2
  165.3 0.0 copy-done.6
  165.3 0.0 copy-start.3
  165.4 0.0 copy-start.5
  165.4 0.0 copy-start.4
  165.4 1.9 multiply_convert_fusion.1
  167.3 0.8 pad_maximum_fusion.1
  168.1 0.9 copy.46.table_ref
  169.0 0.0 copy-done.3
  169.0 1.0 copy.44
  170.0 0.0 copy-done.5
  170.0 0.9 copy.43
  170.9 0.0 copy-done.4
  170.9 0.8 copy.45
  171.8 1.0 fusion.22
  172.7 61.5 %columns.3 = (bf16[8,4,24,16,128]{4,3,2,1,0:T(8,128)(2,1)}, f32[1088,512]{1,0:T(8,128)}) custom-call(bf16[8,4,2,24,16,128]{5,4,3,2,1,0:T(8,128)(2,1)} %bitcast.5.state_ref.cot_ref, bf16[8,4,2,24,16,128]{5,4,3,2,1,0:T(8,128)(2,1)} %bitcast.5.state_ref.cot_ref, bf16[512,384]{1,0:T(8,128)(2,1)} %copy.46.table_ref, ...), custom_call_target="tpu_custom_call" | custom-call | flops 30601641984 | bytes 13893632 | tf_op jit(solution)/shard_map/columns/pallas_call | solution.py:377
  234.3 70.8 %all-to-all-done.2 = bf16[32,2,24,16,128]{4,3,2,1,0:T(8,128)(2,1)} async-done(((bf16[32,2,24,16,128]{4,3,2,1,0:T(8,128)(2,1)}), bf16[32,2,24,16,128]{4,3,2,1,0:T(8,128)(2,1)}, u32[]{:S(2)}, u32[]{:S(2)}) %all-to-all-start.2) | async-done | bytes 6291488 | tf_op jit(solution)/shard_map/all_to_all | solution.py:455
  305.1 3.1 all-to-all-start.1
  308.2 31.6 %columns.4 = (bf16[8,4,24,8,128]{4,3,2,1,0:T(8,128)(2,1)}, f32[1088,512]{1,0:T(8,128)}) custom-call(bf16[8,4,2,24,16,128]{5,4,3,2,1,0:T(8,128)(2,1)} %bitcast.16.state_ref.cot_ref, bf16[8,4,2,24,16,128]{5,4,3,2,1,0:T(8,128)(2,1)} %bitcast.16.state_ref.cot_ref, bf16[512,384]{1,0:T(8,128)(2,1)} %copy.46.table_ref, ...), custom_call_target="tpu_custom_call" | custom-call | flops 15300820992 | bytes 9175040 | tf_op jit(solution)/shard_map/columns/pallas_call | solution.py:377
  339.8 31.6 %columns.5 = (bf16[8,4,24,8,128]{4,3,2,1,0:T(8,128)(2,1)}, f32[1088,512]{1,0:T(8,128)}) custom-call(bf16[8,4,2,24,16,128]{5,4,3,2,1,0:T(8,128)(2,1)} %bitcast.16.state_ref.cot_ref, bf16[8,4,2,24,16,128]{5,4,3,2,1,0:T(8,128)(2,1)} %bitcast.16.state_ref.cot_ref, bf16[512,384]{1,0:T(8,128)(2,1)} %copy.46.table_ref, ...), custom_call_target="tpu_custom_call" | custom-call | flops 15300820992 | bytes 9175040 | tf_op jit(solution)/shard_map/columns/pallas_call | solution.py:377
  371.4 8.0 %all-to-all-done.1 = bf16[32,24,16,128]{3,2,1,0:T(8,128)(2,1)S(1)} async-done(((bf16[32,24,16,128]{3,2,1,0:T(8,128)(2,1)}), bf16[32,24,16,128]{3,2,1,0:T(8,128)(2,1)S(1)}, u32[]{:S(2)}, u32[]{:S(2)}) %all-to-all-start.1) | async-done | bytes 3145760 | tf_op jit(solution)/shard_map/all_to_all | solution.py:455
  379.5 4.0 all-to-all-start.4
  383.5 2.1 dynamic-slice_convert_fusion
  385.6 0.2 collective-permute-start
  385.8 2.1 collective-permute-done
  387.9 1.6 convert_add_fusion
  389.6 0.0 copy-start.2
  389.6 0.9 copy-done.2
  390.5 1.7 collective-permute-start.1
  392.2 14.0 %collective-permute-done.1 = bf16[272,512]{1,0:T(8,128)(2,1)S(1)} collective-permute-done((bf16[272,512]{1,0:T(8,128)(2,1)S(1)}, bf16[272,512]{1,0:T(8,128)(2,1)S(1)}, u32[]{:S(2)}, u32[]{:S(2)}) %collective-permute-start.1) | collective-permute-done | bytes 278560 | tf_op jit(solution)/shard_map/ppermute | solution.py:397
  406.3 1.1 convert_add_fusion.1
  407.4 1.1 collective-permute-start.2
  408.6 5.4 %collective-permute-done.2 = bf16[136,512]{1,0:T(8,128)(2,1)S(1)} collective-permute-done((bf16[136,512]{1,0:T(8,128)(2,1)S(1)}, bf16[136,512]{1,0:T(8,128)(2,1)S(1)}, u32[]{:S(2)}, u32[]{:S(2)}) %collective-permute-start.2) | collective-permute-done | bytes 139296 | tf_op jit(solution)/shard_map/ppermute | solution.py:397
  414.0 0.3 collective-permute-start.3
  414.3 8.0 %collective-permute-done.3 = bf16[136,512]{1,0:T(8,128)(2,1)S(1)} collective-permute-done((bf16[136,512]{1,0:T(8,128)(2,1)S(1)}, bf16[136,512]{1,0:T(8,128)(2,1)S(1)}, u32[]{:S(2)}, u32[]{:S(2)}) %collective-permute-start.3) | collective-permute-done | bytes 139296 | tf_op jit(solution)/shard_map/ppermute | solution.py:397
  422.4 0.1 collective-permute-start.4
  422.5 0.0 all-to-all-done.4
  422.5 3.4 all-to-all-start.3
  425.9 4.9 %collective-permute-done.4 = bf16[136,512]{1,0:T(8,128)(2,1)S(1)} collective-permute-done((bf16[136,512]{1,0:T(8,128)(2,1)S(1)}, bf16[136,512]{1,0:T(8,128)(2,1)S(1)}, u32[]{:S(2)}, u32[]{:S(2)}) %collective-permute-start.4) | collective-permute-done | bytes 139296 | tf_op jit(solution)/shard_map/ppermute | solution.py:397
  430.8 0.1 collective-permute-start.5
  430.9 8.5 %collective-permute-done.5 = bf16[136,512]{1,0:T(8,128)(2,1)S(1)} collective-permute-done((bf16[136,512]{1,0:T(8,128)(2,1)S(1)}, bf16[136,512]{1,0:T(8,128)(2,1)S(1)}, u32[]{:S(2)}, u32[]{:S(2)}) %collective-permute-start.5) | collective-permute-done | bytes 139296 | tf_op jit(solution)/shard_map/ppermute | solution.py:397
  439.5 4.7 collective-permute-start.6
  444.2 9.4 %collective-permute-done.6 = bf16[272,512]{1,0:T(8,128)(2,1)S(1)} collective-permute-done((bf16[272,512]{1,0:T(8,128)(2,1)S(1)}, bf16[272,512]{1,0:T(8,128)(2,1)S(1)}, u32[]{:S(2)}, u32[]{:S(2)}) %collective-permute-start.6) | collective-permute-done | bytes 278560 | tf_op jit(solution)/shard_map/ppermute | solution.py:397
  453.6 0.1 broadcast_select_fusion.3
  453.7 0.1 collective-permute-start.7
  453.9 1.9 collective-permute-done.7
  455.7 0.2 broadcast_select_fusion.1
  455.9 0.3 convert_multiply_fusion
  456.3 1.0 slice.27
  457.3 0.6 slice.24
  457.9 0.9 slice_bitcast_fusion
  458.7 1.0 copy.50
  459.7 0.6 fusion.32
  460.3 4.5 all-to-all-done.3
  464.9 10.6 %inverse_legendre.1 = f32[16416,128]{1,0:T(8,128)} custom-call(s32[24]{0:T(128)} %dynamic_slice.21.waves, bf16[16416,128]{1,0:T(8,128)(2,1)} %bitcast.30, bf16[24,171,256]{2,1,0:T(8,128)(2,1)} %copy.49.leg_ref, f32[171,1]{1,0:T(8,128)} %fusion.28.factor_ref, bf16[8,4,24,16,128]{4,3,2,1,0:T(8,128)(2,1)} %bitcast.35, ...), custom_call_target="tpu_custom_call" | custom-call | flops 1075838976 | bytes 21000192 | tf_op jit(solution)/shard_map/inverse_legendre/pallas_call | solution.py:179
  (16 shorter events, 0.3 us)
Async XLA Ops:
  14.4 7.5 %copy-start.1 = (bf16[24,171,256]{2,0,1:T(8,128)(2,1)S(1)}, bf16[24,171,256]{2,0,1:T(8,128)(2,1)}, u32[]{:S(2)}) copy-start(bf16[24,171,256]{2,0,1:T(8,128)(2,1)} %param.13) | copy-start | bytes 6303748
  14.4 147.2 %all-to-all-start = ((bf16[32,2,24,16,128]{4,3,2,1,0:T(8,128)(2,1)}), bf16[32,2,24,16,128]{4,3,2,1,0:T(8,128)(2,1)}, u32[]{:S(2)}, u32[]{:S(2)}) async-start(bf16[32,2,24,16,128]{4,3,2,1,0:T(8,128)(2,1)} %bitcast.32), calls=%async_computation | async-start | bytes 12582912 | tf_op jit(solution)/shard_map/all_to_all | solution.py:455
  161.6 3.8 copy-start.6
  161.6 143.5 %all-to-all-start.2 = ((bf16[32,2,24,16,128]{4,3,2,1,0:T(8,128)(2,1)}), bf16[32,2,24,16,128]{4,3,2,1,0:T(8,128)(2,1)}, u32[]{:S(2)}, u32[]{:S(2)}) async-start(bf16[32,2,24,16,128]{4,3,2,1,0:T(8,128)(2,1)} %bitcast.31), calls=%async_computation.2 | async-start | bytes 12582912 | tf_op jit(solution)/shard_map/all_to_all | solution.py:455
  165.3 3.7 copy-start.3
  165.4 4.7 copy-start.5
  165.4 5.5 %copy-start.4 = (bf16[512,256]{1,0:T(8,128)(2,1)S(1)}, bf16[512,256]{1,0:T(8,128)(2,1)}, u32[]{:S(2)}) copy-start(bf16[512,256]{1,0:T(8,128)(2,1)} %param.21) | copy-start | bytes 786436
  305.1 74.4 %all-to-all-start.1 = ((bf16[32,24,16,128]{3,2,1,0:T(8,128)(2,1)}), bf16[32,24,16,128]{3,2,1,0:T(8,128)(2,1)S(1)}, u32[]{:S(2)}, u32[]{:S(2)}) async-start(bf16[32,24,16,128]{3,2,1,0:T(8,128)(2,1)} %bitcast.38), calls=%async_computation.1 | async-start | bytes 6291456 | tf_op jit(solution)/shard_map/all_to_all | solution.py:455
  379.5 10.1 %copy-start = (bf16[32,24,16,128]{3,2,1,0:T(8,128)(2,1)}, bf16[32,24,16,128]{3,2,1,0:T(8,128)(2,1)S(1)}, u32[]{:S(2)}) copy-start(bf16[32,24,16,128]{3,2,1,0:T(8,128)(2,1)S(1)} %all-to-all-done.1) | copy-start | bytes 9437188
  379.5 43.0 %all-to-all-start.4 = ((bf16[32,24,8,128]{3,2,1,0:T(8,128)(2,1)}), bf16[32,24,8,128]{3,2,1,0:T(8,128)(2,1)}, u32[]{:S(2)}, u32[]{:S(2)}) async-start(bf16[32,24,8,128]{3,2,1,0:T(8,128)(2,1)} %bitcast.39), calls=%async_computation.4 | async-start | bytes 3145728 | tf_op jit(solution)/shard_map/all_to_all | solution.py:455
  385.6 2.3 collective-permute-start
  389.6 1.0 copy-start.2
  390.5 15.7 %collective-permute-start.1 = (bf16[272,512]{1,0:T(8,128)(2,1)S(1)}, bf16[272,512]{1,0:T(8,128)(2,1)S(1)}, u32[]{:S(2)}, u32[]{:S(2)}) collective-permute-start(bf16[272,512]{1,0:T(8,128)(2,1)S(1)} %dynamic-slice_convert_fusion.1), channel_id=1, source_target_pairs={{0,2},{1,3},{2,0},{3,1},{4,6},{5,7},{6,4},{7,5},{8,10},{9,11},{10,... | collective-permute-start | bytes 835592 | tf_op jit(solution)/shard_map/ppermute | solution.py:397
  407.4 6.5 %collective-permute-start.2 = (bf16[136,512]{1,0:T(8,128)(2,1)S(1)}, bf16[136,512]{1,0:T(8,128)(2,1)S(1)}, u32[]{:S(2)}, u32[]{:S(2)}) collective-permute-start(bf16[136,512]{1,0:T(8,128)(2,1)S(1)} %dynamic-slice_convert_fusion.2), channel_id=1, source_target_pairs={{0,4},{4,0},{8,12},{12,8},{16,20},{20,16},{24,28},{28,24},{1,5},{5... | collective-permute-start | bytes 417800 | tf_op jit(solution)/shard_map/ppermute | solution.py:397
  414.0 8.4 %collective-permute-start.3 = (bf16[136,512]{1,0:T(8,128)(2,1)S(1)}, bf16[136,512]{1,0:T(8,128)(2,1)S(1)}, u32[]{:S(2)}, u32[]{:S(2)}) collective-permute-start(bf16[136,512]{1,0:T(8,128)(2,1)S(1)} %add_convert_fusion.2), channel_id=1, source_target_pairs={{0,8},{4,12},{8,0},{12,4},{16,24},{20,28},{24,16},{28,20},{1,9},{5... | collective-permute-start | bytes 417800 | tf_op jit(solution)/shard_map/ppermute | solution.py:397
  422.4 8.4 %collective-permute-start.4 = (bf16[136,512]{1,0:T(8,128)(2,1)S(1)}, bf16[136,512]{1,0:T(8,128)(2,1)S(1)}, u32[]{:S(2)}, u32[]{:S(2)}) collective-permute-start(bf16[136,512]{1,0:T(8,128)(2,1)S(1)} %add_convert_fusion.1), channel_id=1, source_target_pairs={{0,16},{4,20},{8,24},{12,28},{16,0},{20,4},{24,8},{28,12},{1,17},{... | collective-permute-start | bytes 417800 | tf_op jit(solution)/shard_map/ppermute | solution.py:397
  422.5 42.4 %all-to-all-start.3 = ((bf16[32,24,8,128]{3,2,1,0:T(8,128)(2,1)}), bf16[32,24,8,128]{3,2,1,0:T(8,128)(2,1)}, u32[]{:S(2)}, u32[]{:S(2)}) async-start(bf16[32,24,8,128]{3,2,1,0:T(8,128)(2,1)} %bitcast.17), calls=%async_computation.3 | async-start | bytes 3145728 | tf_op jit(solution)/shard_map/all_to_all | solution.py:455
  430.8 8.6 %collective-permute-start.5 = (bf16[136,512]{1,0:T(8,128)(2,1)S(1)}, bf16[136,512]{1,0:T(8,128)(2,1)S(1)}, u32[]{:S(2)}, u32[]{:S(2)}) collective-permute-start(bf16[136,512]{1,0:T(8,128)(2,1)S(1)} %add_convert_fusion), channel_id=1, source_target_pairs={{0,4},{4,0},{8,12},{12,8},{16,20},{20,16},{24,28},{28,24},{1,5},{5... | collective-permute-start | bytes 417800 | tf_op jit(solution)/shard_map/ppermute | solution.py:397
  439.5 14.0 %collective-permute-start.6 = (bf16[272,512]{1,0:T(8,128)(2,1)S(1)}, bf16[272,512]{1,0:T(8,128)(2,1)S(1)}, u32[]{:S(2)}, u32[]{:S(2)}) collective-permute-start(bf16[272,512]{1,0:T(8,128)(2,1)S(1)} %pad_maximum_fusion.2), channel_id=1, source_target_pairs={{0,2},{1,3},{2,0},{3,1},{4,6},{5,7},{6,4},{7,5},{8,10},{9,11},{10,... | collective-permute-start | bytes 835592 | tf_op jit(solution)/shard_map/ppermute | solution.py:397
  453.7 2.0 collective-permute-start.7
